TPU v7x, 256 devices: a whole 4x4x8 slice. The times are simulated.
256 devices in a mesh: layer: 32 (over x, z), plane: 8 (over y, core).
Axes of the slice: x: 4, y: 4, z: 8, core: 2. Of those that a mesh axis runs over, the one named last changes fastest.
Arguments:
- sources: float32 [32, 16, 8192], P('layer', None, 'plane'), may hold values from -6 to 6
- fronts: float32 [32, 64, 128, 128], P('layer', 'plane'), as said below
- down_left: bfloat16 [32, 8, 128, 8192], P('layer', None, None, 'plane'), may hold values from -0.1875 to 0.1875
- down_right: bfloat16 [32, 8, 128, 8192], P('layer', None, None, 'plane'), may hold values from -0.25 to 0.25
- up_left: bfloat16 [32, 8, 128, 8192], P('layer', None, None, 'plane'), may hold values from -0.1875 to 0.1875
- up_right: bfloat16 [32, 8, 128, 8192], P('layer', None, None, 'plane'), may hold values from -0.25 to 0.25
- ranks: int32 [32, 2, 8, 8], P('layer', None, 'plane'), may hold values from 1 to 128
- pattern: int32 [32, 2, 8, 8], P('layer', None, 'plane'), may hold values 0 or 1
Outputs:
- field: float32 [32, 16, 8192], P('layer', None, 'plane')
Inputs may be any that keep to these rules, and one draw needn't show every extreme that they name: fronts[l, b] is lower triangular with every diagonal entry between 1 and 4.
All inputs are finite; a program needn't handle non-finite values. No bound on the sum of `pattern` on one device may be relied on, other than what follows from the above.
Results may differ from a plain program's by a relative error of at most 0.025.
Values may be sent and summed in bfloat16 or wider, within the bound.
A program may use at most 64 MiB of HBM per device.

v0:
```python
import jax
import jax.numpy as jnp
from jax import lax
from jax.sharding import PartitionSpec as P


def shifted(value, axis, by):
    length = lax.axis_size(axis)
    pairs = [(i, i + by) for i in range(length) if 0 <= i + by < length]
    return lax.ppermute(value, axis, pairs)


def side_by_side(arrays, axis, split_dim, concat_dim, along):
    ends, at = ([], 0)
    for a in arrays[:-1]:
        at += a.shape[along]
        ends.append(at)
    both = jnp.concatenate(arrays, axis=along)
    return tuple(
        jnp.split(
            lax.all_to_all(both, axis, split_axis=split_dim, concat_axis=concat_dim, tiled=True),
            ends,
            axis=along,
        )
    )


def front_solve(source, front_blocks):
    stacked = source.reshape(
        source.shape[0], front_blocks.shape[0], front_blocks.shape[1]
    ).transpose(1, 2, 0)
    solved = jax.scipy.linalg.solve_triangular(front_blocks, stacked, lower=True)
    return solved.transpose(2, 0, 1).reshape(source.shape)


def compress(trace, factor_in):
    return jnp.einsum(
        "ikt,st->isk", factor_in, trace.astype(jnp.bfloat16), preferred_element_type=jnp.float32
    ).astype(jnp.bfloat16)


def expand(coeffs, factor_out, keep_mask):
    return jnp.einsum(
        "jsk,jkt->st",
        coeffs * keep_mask[:, None, :],
        factor_out,
        preferred_element_type=jnp.float32,
    )


def shards(sources, fronts, down_left, down_right, up_left, up_right, ranks, pattern):
    solved = front_solve(sources[0], fronts[0])
    layer_count = lax.axis_size("layer")
    layer_at = lax.axis_index("layer")
    group_count = 1
    group_rows = solved.shape[0] // group_count
    total_turns = layer_count + group_count - 1
    rank_top = down_left.shape[2]
    ladder = jnp.arange(rank_top, dtype=jnp.int32)
    keep_mask = (
        pattern[0, :, 0, :, None]
        * (ladder[None, None, :] < ranks[0, :, 0, :, None]).astype(jnp.int32)
    ).astype(jnp.bfloat16)
    down_factor = down_left[0]
    up_factor = up_left[0]

    def advance(step_at, carry):
        down_last, up_last, down_all, up_all = carry
        down_in = shifted(down_last.astype(jnp.bfloat16), "layer", 1).astype(down_last.dtype)
        up_in = shifted(up_last.astype(jnp.bfloat16), "layer", -1).astype(up_last.dtype)
        down_coeffs = compress(down_in, down_factor)
        up_coeffs = compress(up_in, up_factor)
        down_group = step_at - layer_at
        up_group = step_at - (layer_count - 1 - layer_at)
        down_start = jnp.clip(down_group, 0, group_count - 1) * group_rows
        up_start = jnp.clip(up_group, 0, group_count - 1) * group_rows
        arrived = side_by_side((down_coeffs, up_coeffs), "plane", 0, 0, 1)
        down_new = solved + expand(arrived[0], down_right[0], keep_mask[0])
        up_new = solved + expand(arrived[1], up_right[0], keep_mask[1])
        down_valid = (down_group >= 0) & (down_group < group_count)
        up_valid = (up_group >= 0) & (up_group < group_count)
        down_all = jnp.where(down_valid, down_new, down_all)
        up_all = jnp.where(up_valid, up_new, up_all)
        return (down_new, up_new, down_all, up_all)

    empty_group = jnp.zeros((group_rows, solved.shape[1]), jnp.float32)
    empty_all = jnp.zeros(solved.shape, jnp.float32)
    _, _, down_all, up_all = lax.fori_loop(
        0, total_turns, advance, (empty_group, empty_group, empty_all, empty_all)
    )
    field = down_all + up_all - solved
    return field[None]


def solution(mesh):
    in_specs = (
        P("layer", None, "plane"),
        P("layer", "plane", None, None),
        P("layer", None, None, "plane"),
        P("layer", None, None, "plane"),
        P("layer", None, None, "plane"),
        P("layer", None, None, "plane"),
        P("layer", None, "plane", None),
        P("layer", None, "plane", None),
    )
    out_specs = P("layer", None, "plane")
    return jax.shard_map(shards, mesh=mesh, in_specs=in_specs, out_specs=out_specs, check_vma=False)
```

profile of v0, /device:TPU:6, one launch (start us, length us, event | category | flops | bytes accessed | tf_op | source)
XLA Modules:
  0.0 829.2 jit_solution(9556106407661515722)
XLA Ops:
  1.1 78.6 %custom-call.4 = f32[8,1,128,128]{2,3,1,0:T(8,128)S(1)} custom-call(f32[8,1,128,128]{3,2,1,0:T(8,128)S(1)} %select_bitcast_fusion), custom_call_target="InvertDiagBlocksLowerTriangular" | custom-call | tf_op jit(solution)/shard_map/jit(_solve_triangular)/vmap()/triangular_solve | solution.py:32
  82.0 746.6 %while.21 = (s32[]{:T(128)}, bf16[16,1024]{1,0:T(8,128)(2,1)S(1)}, bf16[16,1024]{1,0:T(8,128)(2,1)S(1)}, f32[16,1024]{1,0:T(8,128)S(1)}, f32[16,1024]{1,0:T(8,12...) while((s32[]{:T(128)}, bf16[16,1024]{1,0:T(8,128)(2,1)S(1)}, ...), condition=%wide.region_1.2_spmd.clone, body=%wide.region_0.1_spmd.clone.sunk | while | flops 134578176 | bytes 26554760 | solution.py:88
  82.0 8.2 collective-permute-start
  94.3 3.7 collective-permute-done.1
  99.4 4.6 all-to-all-start
  104.0 5.6 all-to-all-done
  114.5 3.5 collective-permute-start.1
  127.2 5.5 all-to-all-done
  137.6 3.5 collective-permute-start.1
  150.3 5.5 all-to-all-done
  160.7 3.5 collective-permute-start.1
  173.4 5.5 all-to-all-done
  183.8 3.5 collective-permute-start.1
  196.6 5.5 all-to-all-done
  206.9 3.5 collective-permute-start.1
  219.7 5.5 all-to-all-done
  230.1 3.5 collective-permute-start.1
  242.8 5.5 all-to-all-done
  253.2 3.5 collective-permute-start.1
  265.9 5.5 all-to-all-done
  276.3 3.5 collective-permute-start.1
  289.0 5.5 all-to-all-done
  299.4 3.5 collective-permute-start.1
  312.1 5.5 all-to-all-done
  322.5 3.5 collective-permute-start.1
  335.3 5.5 all-to-all-done
  345.6 3.5 collective-permute-start.1
  358.4 5.5 all-to-all-done
  368.7 3.5 collective-permute-start.1
  381.5 5.5 all-to-all-done
  391.9 3.5 collective-permute-start.1
  404.6 5.5 all-to-all-done
  415.0 3.5 collective-permute-start.1
  427.7 5.5 all-to-all-done
  438.1 3.5 collective-permute-start.1
  450.8 5.5 all-to-all-done
  461.2 3.5 collective-permute-start.1
  473.9 5.5 all-to-all-done
  497.1 5.5 all-to-all-done
  507.4 3.5 collective-permute-start.1
  520.2 5.5 all-to-all-done
  530.6 3.5 collective-permute-start.1
  543.3 5.5 all-to-all-done
  553.7 3.5 collective-permute-start.1
  566.4 5.5 all-to-all-done
  576.8 3.5 collective-permute-start.1
  589.5 5.5 all-to-all-done
  599.9 3.5 collective-permute-start.1
  612.6 5.5 all-to-all-done
  623.0 3.5 collective-permute-start.1
  635.8 5.5 all-to-all-done
  646.1 3.5 collective-permute-start.1
  658.9 5.5 all-to-all-done
  669.3 3.5 collective-permute-start.1
  682.0 5.5 all-to-all-done
  705.1 5.5 all-to-all-done
  715.5 3.5 collective-permute-start.1
  728.2 5.5 all-to-all-done
  751.3 5.5 all-to-all-done
  761.7 3.5 collective-permute-start.1
  774.5 5.5 all-to-all-done
  797.6 5.5 all-to-all-done
  807.9 3.5 collective-permute-start.1
  820.7 5.5 all-to-all-done
  (525 shorter events, 459.8 us)
Async XLA Ops:
  82.0 10.1 %collective-permute-start = (bf16[16,1024]{1,0:T(8,128)(2,1)S(1)}, bf16[16,1024]{1,0:T(8,128)(2,1)S(1)}, u32[]{:S(2)}, u32[]{:S(2)}) collective-permute-start(bf16[16,1024]{1,0:T(8,128)(2,1)S(1)} %select_convert_fusion.5), channel_id=1, source_target_pairs={{8,0},{16,8},{24,16},{32,24},{40,32},{48,40},{56,48},{64,56},{72,6... | collective-permute-start | bytes 98312 | tf_op jit(solution)/shard_map/while/body/eval_jaxpr/ppermute | solution.py:10
  90.2 7.9 collective-permute-start.1
  99.4 10.2 %all-to-all-start = ((bf16[8,32,128]{2,1,0:T(8,128)(2,1)}), bf16[8,32,128]{2,1,0:T(8,128)(2,1)S(1)}, u32[]{:S(2)}, u32[]{:S(2)}) async-start(bf16[8,32,128]{2,1,0:T(8,128)(2,1)} %pad_maximum_fusion.2), calls=%async_computation | async-start | bytes 131072 | tf_op jit(solution)/shard_map/while/body/eval_jaxpr/all_to_all | solution.py:21
  114.5 7.9 collective-permute-start.1
  123.7 9.0 %all-to-all-start = ((bf16[8,32,128]{2,1,0:T(8,128)(2,1)}), bf16[8,32,128]{2,1,0:T(8,128)(2,1)S(1)}, u32[]{:S(2)}, u32[]{:S(2)}) async-start(bf16[8,32,128]{2,1,0:T(8,128)(2,1)} %pad_maximum_fusion.2), calls=%async_computation | async-start | bytes 131072 | tf_op jit(solution)/shard_map/while/body/eval_jaxpr/all_to_all | solution.py:21
  137.6 7.9 collective-permute-start.1
  146.8 9.0 %all-to-all-start = ((bf16[8,32,128]{2,1,0:T(8,128)(2,1)}), bf16[8,32,128]{2,1,0:T(8,128)(2,1)S(1)}, u32[]{:S(2)}, u32[]{:S(2)}) async-start(bf16[8,32,128]{2,1,0:T(8,128)(2,1)} %pad_maximum_fusion.2), calls=%async_computation | async-start | bytes 131072 | tf_op jit(solution)/shard_map/while/body/eval_jaxpr/all_to_all | solution.py:21
  160.7 7.9 collective-permute-start.1
  169.9 9.0 %all-to-all-start = ((bf16[8,32,128]{2,1,0:T(8,128)(2,1)}), bf16[8,32,128]{2,1,0:T(8,128)(2,1)S(1)}, u32[]{:S(2)}, u32[]{:S(2)}) async-start(bf16[8,32,128]{2,1,0:T(8,128)(2,1)} %pad_maximum_fusion.2), calls=%async_computation | async-start | bytes 131072 | tf_op jit(solution)/shard_map/while/body/eval_jaxpr/all_to_all | solution.py:21
  183.8 7.9 collective-permute-start.1
  193.0 9.0 %all-to-all-start = ((bf16[8,32,128]{2,1,0:T(8,128)(2,1)}), bf16[8,32,128]{2,1,0:T(8,128)(2,1)S(1)}, u32[]{:S(2)}, u32[]{:S(2)}) async-start(bf16[8,32,128]{2,1,0:T(8,128)(2,1)} %pad_maximum_fusion.2), calls=%async_computation | async-start | bytes 131072 | tf_op jit(solution)/shard_map/while/body/eval_jaxpr/all_to_all | solution.py:21
  206.9 7.9 collective-permute-start.1
  216.2 9.0 %all-to-all-start = ((bf16[8,32,128]{2,1,0:T(8,128)(2,1)}), bf16[8,32,128]{2,1,0:T(8,128)(2,1)S(1)}, u32[]{:S(2)}, u32[]{:S(2)}) async-start(bf16[8,32,128]{2,1,0:T(8,128)(2,1)} %pad_maximum_fusion.2), calls=%async_computation | async-start | bytes 131072 | tf_op jit(solution)/shard_map/while/body/eval_jaxpr/all_to_all | solution.py:21
  230.1 7.9 collective-permute-start.1
  239.3 9.0 %all-to-all-start = ((bf16[8,32,128]{2,1,0:T(8,128)(2,1)}), bf16[8,32,128]{2,1,0:T(8,128)(2,1)S(1)}, u32[]{:S(2)}, u32[]{:S(2)}) async-start(bf16[8,32,128]{2,1,0:T(8,128)(2,1)} %pad_maximum_fusion.2), calls=%async_computation | async-start | bytes 131072 | tf_op jit(solution)/shard_map/while/body/eval_jaxpr/all_to_all | solution.py:21
  253.2 7.9 collective-permute-start.1
  262.4 9.0 %all-to-all-start = ((bf16[8,32,128]{2,1,0:T(8,128)(2,1)}), bf16[8,32,128]{2,1,0:T(8,128)(2,1)S(1)}, u32[]{:S(2)}, u32[]{:S(2)}) async-start(bf16[8,32,128]{2,1,0:T(8,128)(2,1)} %pad_maximum_fusion.2), calls=%async_computation | async-start | bytes 131072 | tf_op jit(solution)/shard_map/while/body/eval_jaxpr/all_to_all | solution.py:21
  276.3 7.9 collective-permute-start.1
  285.5 9.0 %all-to-all-start = ((bf16[8,32,128]{2,1,0:T(8,128)(2,1)}), bf16[8,32,128]{2,1,0:T(8,128)(2,1)S(1)}, u32[]{:S(2)}, u32[]{:S(2)}) async-start(bf16[8,32,128]{2,1,0:T(8,128)(2,1)} %pad_maximum_fusion.2), calls=%async_computation | async-start | bytes 131072 | tf_op jit(solution)/shard_map/while/body/eval_jaxpr/all_to_all | solution.py:21
  299.4 7.9 collective-permute-start.1
  308.6 9.0 %all-to-all-start = ((bf16[8,32,128]{2,1,0:T(8,128)(2,1)}), bf16[8,32,128]{2,1,0:T(8,128)(2,1)S(1)}, u32[]{:S(2)}, u32[]{:S(2)}) async-start(bf16[8,32,128]{2,1,0:T(8,128)(2,1)} %pad_maximum_fusion.2), calls=%async_computation | async-start | bytes 131072 | tf_op jit(solution)/shard_map/while/body/eval_jaxpr/all_to_all | solution.py:21
  322.5 7.9 collective-permute-start.1
  331.7 9.0 %all-to-all-start = ((bf16[8,32,128]{2,1,0:T(8,128)(2,1)}), bf16[8,32,128]{2,1,0:T(8,128)(2,1)S(1)}, u32[]{:S(2)}, u32[]{:S(2)}) async-start(bf16[8,32,128]{2,1,0:T(8,128)(2,1)} %pad_maximum_fusion.2), calls=%async_computation | async-start | bytes 131072 | tf_op jit(solution)/shard_map/while/body/eval_jaxpr/all_to_all | solution.py:21
  345.6 7.9 collective-permute-start.1
  354.9 9.0 %all-to-all-start = ((bf16[8,32,128]{2,1,0:T(8,128)(2,1)}), bf16[8,32,128]{2,1,0:T(8,128)(2,1)S(1)}, u32[]{:S(2)}, u32[]{:S(2)}) async-start(bf16[8,32,128]{2,1,0:T(8,128)(2,1)} %pad_maximum_fusion.2), calls=%async_computation | async-start | bytes 131072 | tf_op jit(solution)/shard_map/while/body/eval_jaxpr/all_to_all | solution.py:21
  368.7 7.9 collective-permute-start.1
  378.0 9.0 %all-to-all-start = ((bf16[8,32,128]{2,1,0:T(8,128)(2,1)}), bf16[8,32,128]{2,1,0:T(8,128)(2,1)S(1)}, u32[]{:S(2)}, u32[]{:S(2)}) async-start(bf16[8,32,128]{2,1,0:T(8,128)(2,1)} %pad_maximum_fusion.2), calls=%async_computation | async-start | bytes 131072 | tf_op jit(solution)/shard_map/while/body/eval_jaxpr/all_to_all | solution.py:21
  391.9 7.9 collective-permute-start.1
  401.1 9.0 %all-to-all-start = ((bf16[8,32,128]{2,1,0:T(8,128)(2,1)}), bf16[8,32,128]{2,1,0:T(8,128)(2,1)S(1)}, u32[]{:S(2)}, u32[]{:S(2)}) async-start(bf16[8,32,128]{2,1,0:T(8,128)(2,1)} %pad_maximum_fusion.2), calls=%async_computation | async-start | bytes 131072 | tf_op jit(solution)/shard_map/while/body/eval_jaxpr/all_to_all | solution.py:21
  415.0 7.9 collective-permute-start.1
  424.2 9.0 %all-to-all-start = ((bf16[8,32,128]{2,1,0:T(8,128)(2,1)}), bf16[8,32,128]{2,1,0:T(8,128)(2,1)S(1)}, u32[]{:S(2)}, u32[]{:S(2)}) async-start(bf16[8,32,128]{2,1,0:T(8,128)(2,1)} %pad_maximum_fusion.2), calls=%async_computation | async-start | bytes 131072 | tf_op jit(solution)/shard_map/while/body/eval_jaxpr/all_to_all | solution.py:21
  438.1 7.9 collective-permute-start.1
  447.3 9.0 %all-to-all-start = ((bf16[8,32,128]{2,1,0:T(8,128)(2,1)}), bf16[8,32,128]{2,1,0:T(8,128)(2,1)S(1)}, u32[]{:S(2)}, u32[]{:S(2)}) async-start(bf16[8,32,128]{2,1,0:T(8,128)(2,1)} %pad_maximum_fusion.2), calls=%async_computation | async-start | bytes 131072 | tf_op jit(solution)/shard_map/while/body/eval_jaxpr/all_to_all | solution.py:21
  461.2 7.9 collective-permute-start.1
  470.4 9.0 %all-to-all-start = ((bf16[8,32,128]{2,1,0:T(8,128)(2,1)}), bf16[8,32,128]{2,1,0:T(8,128)(2,1)S(1)}, u32[]{:S(2)}, u32[]{:S(2)}) async-start(bf16[8,32,128]{2,1,0:T(8,128)(2,1)} %pad_maximum_fusion.2), calls=%async_computation | async-start | bytes 131072 | tf_op jit(solution)/shard_map/while/body/eval_jaxpr/all_to_all | solution.py:21
  484.3 7.9 collective-permute-start.1
  493.5 9.0 %all-to-all-start = ((bf16[8,32,128]{2,1,0:T(8,128)(2,1)}), bf16[8,32,128]{2,1,0:T(8,128)(2,1)S(1)}, u32[]{:S(2)}, u32[]{:S(2)}) async-start(bf16[8,32,128]{2,1,0:T(8,128)(2,1)} %pad_maximum_fusion.2), calls=%async_computation | async-start | bytes 131072 | tf_op jit(solution)/shard_map/while/body/eval_jaxpr/all_to_all | solution.py:21
  507.4 7.9 collective-permute-start.1
  516.7 9.0 %all-to-all-start = ((bf16[8,32,128]{2,1,0:T(8,128)(2,1)}), bf16[8,32,128]{2,1,0:T(8,128)(2,1)S(1)}, u32[]{:S(2)}, u32[]{:S(2)}) async-start(bf16[8,32,128]{2,1,0:T(8,128)(2,1)} %pad_maximum_fusion.2), calls=%async_computation | async-start | bytes 131072 | tf_op jit(solution)/shard_map/while/body/eval_jaxpr/all_to_all | solution.py:21
  530.6 7.9 collective-permute-start.1
  539.8 9.0 %all-to-all-start = ((bf16[8,32,128]{2,1,0:T(8,128)(2,1)}), bf16[8,32,128]{2,1,0:T(8,128)(2,1)S(1)}, u32[]{:S(2)}, u32[]{:S(2)}) async-start(bf16[8,32,128]{2,1,0:T(8,128)(2,1)} %pad_maximum_fusion.2), calls=%async_computation | async-start | bytes 131072 | tf_op jit(solution)/shard_map/while/body/eval_jaxpr/all_to_all | solution.py:21
  553.7 7.9 collective-permute-start.1
  562.9 9.0 %all-to-all-start = ((bf16[8,32,128]{2,1,0:T(8,128)(2,1)}), bf16[8,32,128]{2,1,0:T(8,128)(2,1)S(1)}, u32[]{:S(2)}, u32[]{:S(2)}) async-start(bf16[8,32,128]{2,1,0:T(8,128)(2,1)} %pad_maximum_fusion.2), calls=%async_computation | async-start | bytes 131072 | tf_op jit(solution)/shard_map/while/body/eval_jaxpr/all_to_all | solution.py:21
  576.8 7.9 collective-permute-start.1
  586.0 9.0 %all-to-all-start = ((bf16[8,32,128]{2,1,0:T(8,128)(2,1)}), bf16[8,32,128]{2,1,0:T(8,128)(2,1)S(1)}, u32[]{:S(2)}, u32[]{:S(2)}) async-start(bf16[8,32,128]{2,1,0:T(8,128)(2,1)} %pad_maximum_fusion.2), calls=%async_computation | async-start | bytes 131072 | tf_op jit(solution)/shard_map/while/body/eval_jaxpr/all_to_all | solution.py:21
  599.9 7.9 collective-permute-start.1
  609.1 9.0 %all-to-all-start = ((bf16[8,32,128]{2,1,0:T(8,128)(2,1)}), bf16[8,32,128]{2,1,0:T(8,128)(2,1)S(1)}, u32[]{:S(2)}, u32[]{:S(2)}) async-start(bf16[8,32,128]{2,1,0:T(8,128)(2,1)} %pad_maximum_fusion.2), calls=%async_computation | async-start | bytes 131072 | tf_op jit(solution)/shard_map/while/body/eval_jaxpr/all_to_all | solution.py:21
  623.0 7.9 collective-permute-start.1
  632.2 9.0 %all-to-all-start = ((bf16[8,32,128]{2,1,0:T(8,128)(2,1)}), bf16[8,32,128]{2,1,0:T(8,128)(2,1)S(1)}, u32[]{:S(2)}, u32[]{:S(2)}) async-start(bf16[8,32,128]{2,1,0:T(8,128)(2,1)} %pad_maximum_fusion.2), calls=%async_computation | async-start | bytes 131072 | tf_op jit(solution)/shard_map/while/body/eval_jaxpr/all_to_all | solution.py:21
  646.1 7.9 collective-permute-start.1
  655.4 9.0 %all-to-all-start = ((bf16[8,32,128]{2,1,0:T(8,128)(2,1)}), bf16[8,32,128]{2,1,0:T(8,128)(2,1)S(1)}, u32[]{:S(2)}, u32[]{:S(2)}) async-start(bf16[8,32,128]{2,1,0:T(8,128)(2,1)} %pad_maximum_fusion.2), calls=%async_computation | async-start | bytes 131072 | tf_op jit(solution)/shard_map/while/body/eval_jaxpr/all_to_all | solution.py:21
  669.3 7.9 collective-permute-start.1
  678.5 9.0 %all-to-all-start = ((bf16[8,32,128]{2,1,0:T(8,128)(2,1)}), bf16[8,32,128]{2,1,0:T(8,128)(2,1)S(1)}, u32[]{:S(2)}, u32[]{:S(2)}) async-start(bf16[8,32,128]{2,1,0:T(8,128)(2,1)} %pad_maximum_fusion.2), calls=%async_computation | async-start | bytes 131072 | tf_op jit(solution)/shard_map/while/body/eval_jaxpr/all_to_all | solution.py:21
  692.4 7.9 collective-permute-start.1
  701.6 9.0 %all-to-all-start = ((bf16[8,32,128]{2,1,0:T(8,128)(2,1)}), bf16[8,32,128]{2,1,0:T(8,128)(2,1)S(1)}, u32[]{:S(2)}, u32[]{:S(2)}) async-start(bf16[8,32,128]{2,1,0:T(8,128)(2,1)} %pad_maximum_fusion.2), calls=%async_computation | async-start | bytes 131072 | tf_op jit(solution)/shard_map/while/body/eval_jaxpr/all_to_all | solution.py:21
  715.5 7.9 collective-permute-start.1
  724.7 9.0 %all-to-all-start = ((bf16[8,32,128]{2,1,0:T(8,128)(2,1)}), bf16[8,32,128]{2,1,0:T(8,128)(2,1)S(1)}, u32[]{:S(2)}, u32[]{:S(2)}) async-start(bf16[8,32,128]{2,1,0:T(8,128)(2,1)} %pad_maximum_fusion.2), calls=%async_computation | async-start | bytes 131072 | tf_op jit(solution)/shard_map/while/body/eval_jaxpr/all_to_all | solution.py:21
  738.6 7.9 collective-permute-start.1
  747.8 9.0 %all-to-all-start = ((bf16[8,32,128]{2,1,0:T(8,128)(2,1)}), bf16[8,32,128]{2,1,0:T(8,128)(2,1)S(1)}, u32[]{:S(2)}, u32[]{:S(2)}) async-start(bf16[8,32,128]{2,1,0:T(8,128)(2,1)} %pad_maximum_fusion.2), calls=%async_computation | async-start | bytes 131072 | tf_op jit(solution)/shard_map/while/body/eval_jaxpr/all_to_all | solution.py:21
  761.7 7.9 collective-permute-start.1
  770.9 9.0 %all-to-all-start = ((bf16[8,32,128]{2,1,0:T(8,128)(2,1)}), bf16[8,32,128]{2,1,0:T(8,128)(2,1)S(1)}, u32[]{:S(2)}, u32[]{:S(2)}) async-start(bf16[8,32,128]{2,1,0:T(8,128)(2,1)} %pad_maximum_fusion.2), calls=%async_computation | async-start | bytes 131072 | tf_op jit(solution)/shard_map/while/body/eval_jaxpr/all_to_all | solution.py:21
  794.0 9.0 %all-to-all-start = ((bf16[8,32,128]{2,1,0:T(8,128)(2,1)}), bf16[8,32,128]{2,1,0:T(8,128)(2,1)S(1)}, u32[]{:S(2)}, u32[]{:S(2)}) async-start(bf16[8,32,128]{2,1,0:T(8,128)(2,1)} %pad_maximum_fusion.2), calls=%async_computation | async-start | bytes 131072 | tf_op jit(solution)/shard_map/while/body/eval_jaxpr/all_to_all | solution.py:21
  807.9 7.9 collective-permute-start.1
  817.2 9.0 %all-to-all-start = ((bf16[8,32,128]{2,1,0:T(8,128)(2,1)}), bf16[8,32,128]{2,1,0:T(8,128)(2,1)S(1)}, u32[]{:S(2)}, u32[]{:S(2)}) async-start(bf16[8,32,128]{2,1,0:T(8,128)(2,1)} %pad_maximum_fusion.2), calls=%async_computation | async-start | bytes 131072 | tf_op jit(solution)/shard_map/while/body/eval_jaxpr/all_to_all | solution.py:21
  (96 other events, 907.7 us)
where the time goes:
time: 836 us; the launch traced here: 829 us
  starting transfers between devices  308 us (37%)
  waiting for transfers between devices  246 us (29%)
  matrix products  169 us (20%)
  other arithmetic  103 us (12%)
    ppermute x64, starting transfers between devices, shifted(): return lax.ppermute(value, axis, pairs)  195 us
    all_to_all x32, waiting for transfers between devices, side_by_side(): lax.all_to_all(both, axis, split_axis=split_dim, concat_axis=concat_dim,...  176 us
    all_to_all x32, starting transfers between devices, side_by_side(): lax.all_to_all(both, axis, split_axis=split_dim, concat_axis=concat_dim,...  113 us
    dot_general x64, matrix products, compress(): jnp.einsum('ikt,st->isk', factor_in, trace.astype(jnp.bfloat16), preferre...  92.3 us
    another operation x3, other arithmetic, front_solve(): jax.scipy.linalg.solve_triangular(front_blocks, stacked, lower=True)  79.7 us
    dot_general x64, matrix products, expand(): jnp.einsum('jsk,jkt->st', coeffs * keep_mask[:, None, :], factor_out, pre...  75.8 us
    ppermute x64, waiting for transfers between devices, shifted(): return lax.ppermute(value, axis, pairs)  69.9 us
    concatenate x32, other arithmetic, side_by_side(): both = jnp.concatenate(arrays, axis=along)  20.8 us
  transfers between devices with their start and end apart: 96, of which 64 were waited for; matrix products, arithmetic and copies ran while one was open for 9% of the time, Pallas kernels for 0%

commit v1 on v0

v1 whole, which is shorter than its diff:
```python
import jax
import jax.numpy as jnp
from jax import lax
from jax.experimental import pallas as pl
from jax.experimental.pallas import tpu as pltpu
from jax.sharding import PartitionSpec as P

MESH = pl.DeviceIdType.MESH
BF16, F32 = jnp.bfloat16, jnp.float32
LAYERS, CHIPS, SOURCES = 32, 4, 16
LAST = LAYERS - 1
SEND_EARLY, MAKE_EARLY = 8, 10
NT = (((1,), (1,)), ((), ()))


def piece_row(ref):
    return jnp.concatenate([ref[j] for j in range(8)], axis=1)


def kernel(
    sources, fronts, down_left, down_right, up_left, up_right, ranks, pattern, out,
    src, tri, solved, solved_even, solved_odd, kept, even_right, odd_right, even_left, odd_left,
    even_step, odd_step, even_start, odd_start, even_in, odd_in, own_in, sent,
    load_sem, kept_sem, left_sem, solved_sem, sent_sem, relay_sem,
    even_right_got, odd_right_got, even_left_got, solved_even_got, solved_odd_got, even_in_got, odd_in_got, own_in_got, go_sem,
):
    layer, plane = lax.axis_index("layer"), lax.axis_index("plane")
    y, core = plane // 2, lax.rem(plane, 2)
    is_odd = core == 1
    odd_plane = 2 * y + 1
    upper = (layer >= LAYERS // 2).astype(jnp.int32)
    first, second = upper, 1 - upper
    lefts, rights = (down_left, up_left), (down_right, up_right)

    def sign(d):
        return 1 - 2 * d

    def position(d):
        return jnp.where(d == 0, layer, LAST - layer)

    def remote(source, target, send, got, to_layer, to_plane):
        return pltpu.make_async_remote_copy(
            source, target, send, got, device_id=(to_layer, to_plane), device_id_type=MESH
        )

    load_tri = pltpu.make_async_copy(fronts.at[0], tri, load_sem.at[0])
    load_src = pltpu.make_async_copy(sources.at[0], src, load_sem.at[1])
    load_right = [pltpu.make_async_copy(rights[d].at[0], kept.at[d], load_sem.at[2 + d]) for d in range(2)]
    load_left = [pltpu.make_async_copy(lefts[d].at[0], odd_left.at[d], load_sem.at[4 + d]) for d in range(2)]
    for copy in load_right:
        copy.start()
    load_tri.start()
    load_src.start()
    for copy in load_left:
        copy.start()

    barrier = pltpu.get_barrier_semaphore()

    def greet(to_layer, to_plane):
        pl.semaphore_signal(barrier, inc=1, device_id=(to_layer, to_plane), device_id_type=MESH)

    def reach(r):
        return jnp.minimum(layer + r, LAST) - jnp.maximum(layer - r, 0) + 1

    @pl.when(is_odd)
    def _():
        for by in (-2, -1, 1, 2):

            @pl.when((layer + by >= 0) & (layer + by <= LAST))
            def _():
                for other in range(CHIPS):
                    greet(layer + by, 2 * other + 1)

        for turn in range(1, CHIPS):
            greet(layer, 2 * lax.rem(y + turn, CHIPS) + 1)
        for by in (-1, 0, 1):

            @pl.when((layer + by >= 0) & (layer + by <= LAST))
            def _():
                greet(layer + by, 2 * y)

        pl.semaphore_wait(barrier, CHIPS * reach(2) - 1 + reach(1))

    @pl.when(core == 0)
    def _():
        for by in (-1, 0, 1):

            @pl.when((layer + by >= 0) & (layer + by <= LAST))
            def _():
                greet(layer + by, odd_plane)

        pl.semaphore_wait(barrier, reach(1))

    def send_left(d, start):
        for way in range(2):

            @pl.when((core == 0) & (d == way) & (position(way) >= 1))
            def _():
                copy = remote(
                    lefts[way].at[0], even_left.at[way], left_sem.at[way], even_left_got.at[way],
                    layer - sign(way), odd_plane,
                )
                if start:
                    copy.start()
                else:
                    copy.wait_send()

    def send_right(d, start):
        even = remote(kept.at[d], even_right.at[d], kept_sem.at[d], even_right_got.at[d], layer, odd_plane)
        odd = remote(kept.at[d], odd_right.at[d], kept_sem.at[d], odd_right_got.at[d], layer + sign(d), odd_plane)

        @pl.when(core == 0)
        def _():
            if start:
                even.start()
            else:
                even.wait_send()

        @pl.when(is_odd & (position(d) < LAST))
        def _():
            if start:
                odd.start()
            else:
                odd.wait_send()

    def mask_right(d):
        for j in range(8):
            top = ranks[0, d, 0, j] * pattern[0, d, 0, j]
            rows = lax.broadcasted_iota(jnp.int32, (128, 1024), 0)
            kept[d, j] = jnp.where(rows < top, kept[d, j].astype(F32), 0.0).astype(BF16)

    send_left(first, True)
    for copy in load_right:
        copy.wait()
    mask_right(first)
    send_right(first, True)
    mask_right(second)

    load_tri.wait()
    load_src.wait()
    row = lax.broadcasted_iota(jnp.int32, (128, 128), 0)
    col = lax.broadcasted_iota(jnp.int32, (128, 128), 1)

    def exact(a, b):
        return jnp.dot(a, b, preferred_element_type=F32, precision=lax.Precision.HIGHEST)

    for b in range(8):
        block = tri[b]
        diagonal = jnp.where(row == col, block, 0.0)
        by_row = 1.0 / jnp.sum(diagonal, axis=1, keepdims=True)
        by_col = 1.0 / jnp.sum(diagonal, axis=0, keepdims=True)
        unit = jnp.where(row > col, block * by_row, 0.0)
        inverse = jnp.where(row == col, 1.0, 0.0)
        half = 1
        while half < 128:
            joins = (row // (2 * half) == col // (2 * half)) & (row // half != col // half)
            part = jnp.where(joins, unit, 0.0)
            if half == 1:
                inverse = inverse - part
            else:
                inverse = inverse - exact(inverse, exact(part, inverse))
            half *= 2
        scaled = src[:, 128 * b : 128 * (b + 1)] * by_col
        solved[:, 128 * b : 128 * (b + 1)] = lax.dot_general(
            scaled, inverse, NT, preferred_element_type=F32, precision=lax.Precision.HIGHEST
        )
    sent_solved = solved_odd.at[2]
    sent_solved[...] = solved[...].astype(BF16)
    even_solved = remote(sent_solved, solved_even, solved_sem.at[0], solved_even_got, layer, odd_plane)

    def odd_solved(d):
        return remote(
            sent_solved, solved_odd.at[d], solved_sem.at[d], solved_odd_got.at[d], layer + sign(d), odd_plane
        )

    @pl.when(core == 0)
    def _():
        even_solved.start()

    for d in range(2):

        @pl.when(is_odd & (position(d) < LAST))
        def _():
            odd_solved(d).start()

    for copy in load_left:
        copy.wait()
    send_left(first, False)
    send_right(first, False)

    def send_second():
        send_left(second, True)
        send_right(second, True)

    @pl.when(position(first) >= SEND_EARLY)
    def _():
        send_second()

    def make(right, left, d, solution_part, step, start):
        @pl.loop(0, CHIPS)
        def _(chip):
            block = left[d, pl.ds(2 * chip, 2)].reshape(256, 1024)
            full = right[d].reshape(1024, 1024)
            step[d, chip] = lax.dot_general(full, block, NT, preferred_element_type=F32).astype(BF16)
            start[d, chip] = lax.dot_general(solution_part, block, NT, preferred_element_type=F32)

    def prepare(d):
        q = position(d)

        @pl.when(q >= 1)
        def _():
            remote(kept.at[d], odd_right.at[d], kept_sem.at[d], odd_right_got.at[d], layer, odd_plane).wait_recv()
            remote(sent_solved, solved_odd.at[d], solved_sem.at[d], solved_odd_got.at[d], layer, odd_plane).wait_recv()
            make(odd_right, odd_left, d, solved_odd[d], odd_step, odd_start)

        remote(kept.at[d], even_right.at[d], kept_sem.at[d], even_right_got.at[d], layer, odd_plane).wait_recv()

        @pl.when(q < LAST)
        def _():
            remote(even_left.at[d], even_left.at[d], left_sem.at[d], even_left_got.at[d], layer, odd_plane).wait_recv()
            make(even_right, even_left, d, solved_even[...], even_step, even_start)

    def advance(d, event, values, step, start, deliver):
        for turn in (2, 1, 3, 0):
            other = lax.rem(y + turn, CHIPS)
            result = start[d, other]
            if values is not None:
                result = result + jnp.dot(values, step[d, other], preferred_element_type=F32)
            result = result.astype(BF16)
            deliver(turn, other, result)

    def wait_pieces(ref, got, count):
        remote(ref.at[pl.ds(0, count)], ref.at[pl.ds(0, count)], sent_sem.at[0], got, layer, odd_plane).wait_recv()

    def run_odd(d):
        q = position(d)

        def deliver(turn, other, result):
            for part in range(2):
                sent[d, 1, other, part] = result[:, 128 * part : 128 * (part + 1)]
            if turn == 0:
                even_in[d, odd_plane] = result[:, :128]
            else:
                remote(
                    sent.at[d, 1, other, 0], even_in.at[d, odd_plane], sent_sem.at[d], even_in_got.at[d],
                    layer, 2 * other + 1,
                ).start()

            @pl.when(q < LAST)
            def _():
                remote(
                    sent.at[d, 1, other, 1], odd_in.at[d, odd_plane], sent_sem.at[d], odd_in_got.at[d],
                    layer + sign(d), 2 * other + 1,
                ).start()

            @pl.when(q == LAST)
            def _():
                if turn == 0:
                    own_in[d, odd_plane] = result[:, 128:]
                else:
                    remote(
                        sent.at[d, 1, other, 1], own_in.at[d, odd_plane], sent_sem.at[d], own_in_got.at[d],
                        layer, 2 * other + 1,
                    ).start()

        @pl.when(q == 1)
        def _():
            advance(d, 1, None, odd_step, odd_start, deliver)

        @pl.when(q >= 2)
        def _():
            wait_pieces(odd_in.at[d], odd_in_got.at[d], 8)
            advance(d, 1, piece_row(odd_in.at[d]), odd_step, odd_start, deliver)

    def run_even(d):
        q = position(d)

        def deliver(turn, other, result):
            for part in range(2):
                sent[d, 0, other, part] = result[:, 128 * part : 128 * (part + 1)]
            remote(
                sent.at[d, 0, other, 0], even_in.at[d, 2 * y], sent_sem.at[d], even_in_got.at[d],
                layer + sign(d), 2 * other + 1,
            ).start()

            @pl.when(q < LAST - 1)
            def _():
                remote(
                    sent.at[d, 0, other, 1], odd_in.at[d, 2 * y], sent_sem.at[d], odd_in_got.at[d],
                    layer + 2 * sign(d), 2 * other + 1,
                ).start()

            @pl.when(q == LAST - 1)
            def _():
                remote(
                    sent.at[d, 0, other, 1], own_in.at[d, 2 * y], sent_sem.at[d], own_in_got.at[d],
                    layer + sign(d), 2 * other + 1,
                ).start()

        @pl.when(q == 0)
        def _():
            advance(d, 0, None, even_step, even_start, deliver)

        @pl.when(q >= 1)
        def _():
            wait_pieces(even_in.at[d], even_in_got.at[d], 7)

        @pl.when((q >= 1) & (q < LAST))
        def _():
            advance(d, 0, piece_row(even_in.at[d]), even_step, even_start, deliver)

    def relay_even(d):
        return remote(even_in.at[d], own_in.at[d], relay_sem.at[0, d], own_in_got.at[d], layer, 2 * y)

    def relay_odd(d):
        return remote(odd_in.at[d], own_in.at[d], relay_sem.at[1, d], own_in_got.at[d], layer - sign(d), odd_plane)

    def sweep(d):
        q = position(d)
        run_odd(d)
        run_even(d)

        @pl.when(q >= 1)
        def _():
            relay_even(d).start()

        @pl.when(q >= 2)
        def _():
            relay_odd(d).start()

    @pl.when(is_odd)
    def _():
        remote(sent_solved, solved_even, solved_sem.at[0], solved_even_got, layer, odd_plane).wait_recv()
        prepare(first)

        @pl.when(position(first) >= MAKE_EARLY)
        def _():
            prepare(second)

        sweep(first)

        @pl.when(position(first) < SEND_EARLY)
        def _():
            pl.semaphore_signal(go_sem, inc=1, device_id=(layer, 2 * y), device_id_type=MESH)
            send_second()

        @pl.when(position(first) < MAKE_EARLY)
        def _():
            prepare(second)

        sweep(second)

    @pl.when((core == 0) & (position(first) < SEND_EARLY))
    def _():
        pl.semaphore_wait(go_sem, 1)
        send_second()

    def add_own(d):
        q = position(d)

        @pl.when(q >= 1)
        def _():
            @pl.when(is_odd & (q == LAST))
            def _():
                wait_pieces(own_in.at[d], own_in_got.at[d], 7)

            @pl.when((core == 0) | (q < LAST))
            def _():
                wait_pieces(own_in.at[d], own_in_got.at[d], 8)

            solved[...] += jnp.dot(
                piece_row(own_in.at[d]), kept[d].reshape(1024, 1024), preferred_element_type=F32
            )

    add_own(first)
    add_own(second)
    out[0] = solved[...]

    send_left(second, False)
    send_right(second, False)

    @pl.when(core == 0)
    def _():
        even_solved.wait_send()

    @pl.when(is_odd)
    def _():
        for d in range(2):
            q = position(d)

            def drain(count):
                part = odd_in.at[d, pl.ds(0, count)]
                remote(part, part, sent_sem.at[d], odd_in_got.at[d], layer, odd_plane).wait_send()

            @pl.when(q < LAST)
            def _():
                odd_solved(d).wait_send()
                drain(8)

            @pl.when((q >= 1) & (q < LAST))
            def _():
                drain(7)

            @pl.when(q == LAST)
            def _():
                drain(6)

            @pl.when(q >= 1)
            def _():
                relay_even(d).wait_send()

            @pl.when(q >= 2)
            def _():
                relay_odd(d).wait_send()


def shards(*arrays):
    anywhere = pl.BlockSpec(memory_space=pl.ANY)
    scalars = pl.BlockSpec(memory_space=pltpu.SMEM)
    dma, vmem = pltpu.SemaphoreType.DMA, pltpu.VMEM
    return pl.pallas_call(
        kernel,
        name="sweep",
        out_shape=jax.ShapeDtypeStruct((1, SOURCES, 1024), F32),
        in_specs=[anywhere] * 6 + [scalars] * 2,
        out_specs=pl.BlockSpec(memory_space=pltpu.VMEM),
        scratch_shapes=[
            vmem((SOURCES, 1024), F32),
            vmem((8, 128, 128), F32),
            vmem((SOURCES, 1024), F32),
            vmem((SOURCES, 1024), BF16),
            vmem((3, SOURCES, 1024), BF16),
            vmem((2, 8, 128, 1024), BF16),
            vmem((2, 8, 128, 1024), BF16),
            vmem((2, 8, 128, 1024), BF16),
            vmem((2, 8, 128, 1024), BF16),
            vmem((2, 8, 128, 1024), BF16),
            vmem((2, CHIPS, 1024, 256), BF16),
            vmem((2, CHIPS, 1024, 256), BF16),
            vmem((2, CHIPS, SOURCES, 256), F32),
            vmem((2, CHIPS, SOURCES, 256), F32),
            vmem((2, 8, SOURCES, 128), BF16),
            vmem((2, 8, SOURCES, 128), BF16),
            vmem((2, 8, SOURCES, 128), BF16),
            vmem((2, 2, CHIPS, 2, SOURCES, 128), BF16),
            dma((6,)),
            dma((2,)),
            dma((2,)),
            dma((2,)),
            dma((2,)),
            dma((2, 2)),
            dma((2,)),
            dma((2,)),
            dma((2,)),
            dma(()),
            dma((2,)),
            dma((2,)),
            dma((2,)),
            dma((2,)),
            pltpu.SemaphoreType.REGULAR,
        ],
        compiler_params=pltpu.CompilerParams(
            collective_id=0, has_side_effects=True, vmem_limit_bytes=56 << 20
        ),
    )(*arrays)


def solution(mesh):
    in_specs = (
        P("layer", None, "plane"),
        P("layer", "plane", None, None),
        P("layer", None, None, "plane"),
        P("layer", None, None, "plane"),
        P("layer", None, None, "plane"),
        P("layer", None, None, "plane"),
        P("layer", None, "plane", None),
        P("layer", None, "plane", None),
    )
    return jax.shard_map(
        shards, mesh=mesh, in_specs=in_specs, out_specs=P("layer", None, "plane"), check_vma=False
    )
```

time: 836 us -> 158 us (0.19)
  the two profiles are of different devices: /device:TPU:6 before, /device:TPU:1 now
where the time goes in v1:
time: 158 us
  Pallas kernels  156 us (99%)
    pallas_call x1, Pallas kernels, shards(): pl.pallas_call(kernel, name='sweep', out_shape=jax.ShapeDtypeStruct((1, S...  156 us

profile of v1, /device:TPU:1, one launch (start us, length us, event | category | flops | bytes accessed | tf_op | source)
XLA Modules:
  0.0 157.6 jit_solution(7702601942263553013)
XLA Ops:
  0.0 156.1 %sweep.1 = f32[1,16,1024]{2,1,0:T(8,128)} custom-call(f32[1,16,1024]{2,1,0:T(8,128)} %sources.1, f32[1,8,128,128]{3,2,1,0:T(8,128)} %fronts.1, bf16[1,8,128,1024]{3,2,1,0:T(8,128)(2,1)} %down_left.1, bf16[1,8,128,1024]{3,2,1,0:T(8,128)(2,1)} %down_right.1, bf16[1,8,128,1024]{3,2,1,0:T(8,128)(2,1)} %up_left.1, bf16[1,8,128,1024]{3,2,1,0:T(8,128)(2,1)} %up_right.1, ...), custom_call_target="tpu_custom_call" | custom-call | tf_op jit(solution)/shard_map/sweep/pallas_call | solution.py:421
  156.1 1.5 copy.10

commit v2 on v1

v2 whole, which is shorter than its diff:
```python
import jax
import jax.numpy as jnp
from jax import lax
from jax.experimental import pallas as pl
from jax.experimental.pallas import tpu as pltpu
from jax.sharding import PartitionSpec as P

MESH = pl.DeviceIdType.MESH
BF16, F32 = jnp.bfloat16, jnp.float32
LAYERS, CHIPS, SOURCES = 32, 4, 16
LAST = LAYERS - 1
SEND_EARLY, MAKE_EARLY = 11, 14
SLOW = 3
NT = (((1,), (1,)), ((), ()))


def piece_row(ref):
    return jnp.concatenate([ref[j] for j in range(8)], axis=1)


def kernel(
    sources, fronts, down_left, down_right, up_left, up_right, ranks, pattern, out,
    src, tri, solved, solved_even, solved_odd, kept, even_right, odd_right, even_left, odd_left,
    even_step, odd_step, even_start, odd_start, even_in, odd_in, own_in, sent,
    slow_sent, load_sem, kept_sem, left_sem, solved_sem, sent_sem, relay_sem, slow_sem,
    even_right_got, odd_right_got, even_left_got, solved_even_got, solved_odd_got, even_in_got, odd_in_got, own_in_got, go_sem,
):
    layer, plane = lax.axis_index("layer"), lax.axis_index("plane")
    y, core = plane // 2, lax.rem(plane, 2)
    is_odd = core == 1
    odd_plane = 2 * y + 1
    upper = (layer >= LAYERS // 2).astype(jnp.int32)
    first, second = upper, 1 - upper
    lefts, rights = (down_left, up_left), (down_right, up_right)

    def sign(d):
        return 1 - 2 * d

    def position(d):
        return jnp.where(d == 0, layer, LAST - layer)

    def remote(source, target, send, got, to_layer, to_plane):
        return pltpu.make_async_remote_copy(
            source, target, send, got, device_id=(to_layer, to_plane), device_id_type=MESH
        )

    load_tri = pltpu.make_async_copy(fronts.at[0], tri, load_sem.at[0])
    load_src = pltpu.make_async_copy(sources.at[0], src, load_sem.at[1])
    def each(d, action):
        for way in range(2):
            pl.when(d == way)(lambda: action(way))

    def load_right(way):
        return pltpu.make_async_copy(rights[way].at[0], kept.at[way], load_sem.at[2 + way])

    def load_left(way):
        return pltpu.make_async_copy(lefts[way].at[0], odd_left.at[way], load_sem.at[4 + way])

    each(first, lambda way: load_right(way).start())
    load_tri.start()
    load_src.start()

    early = position(first)
    forward = sign(first)
    is_slow = (early >= 1) & (early <= SLOW)

    @pl.when(is_odd | is_slow)
    def _():
        each(first, lambda way: load_left(way).start())

    barrier = pltpu.get_barrier_semaphore()

    def greet(to_layer, to_plane):
        pl.semaphore_signal(barrier, inc=1, device_id=(to_layer, to_plane), device_id_type=MESH)

    def reach(r):
        return jnp.minimum(layer + r, LAST) - jnp.maximum(layer - r, 0) + 1

    @pl.when(is_odd)
    def _():
        for by in (-2, -1, 1, 2):

            @pl.when((layer + by >= 0) & (layer + by <= LAST))
            def _():
                for other in range(CHIPS):
                    greet(layer + by, 2 * other + 1)

        for turn in range(1, CHIPS):
            greet(layer, 2 * lax.rem(y + turn, CHIPS) + 1)
        for by in (-1, 0, 1):

            @pl.when((layer + by >= 0) & (layer + by <= LAST))
            def _():
                greet(layer + by, 2 * y)

        beside_slow = is_slow.astype(jnp.int32)
        past_slow = ((early >= 2) & (early <= SLOW + 1)).astype(jnp.int32)
        for turn in range(1, CHIPS):

            @pl.when(is_slow)
            def _():
                greet(layer, 2 * lax.rem(y + turn, CHIPS))

            @pl.when((early >= 2) & (early <= SLOW + 1))
            def _():
                greet(layer - forward, 2 * lax.rem(y + turn, CHIPS))

        pl.semaphore_wait(barrier, CHIPS * reach(2) - 1 + reach(1) + (CHIPS - 1) * (beside_slow + past_slow))

    @pl.when(core == 0)
    def _():
        for by in (-1, 0, 1):

            @pl.when((layer + by >= 0) & (layer + by <= LAST))
            def _():
                greet(layer + by, odd_plane)

        @pl.when(is_slow)
        def _():
            for turn in range(1, CHIPS):
                greet(layer, 2 * lax.rem(y + turn, CHIPS) + 1)
                greet(layer + forward, 2 * lax.rem(y + turn, CHIPS) + 1)

        @pl.when(early == 0)
        def _():
            greet(layer + forward, plane)

        @pl.when(early == 1)
        def _():
            greet(layer - forward, plane)

        pl.semaphore_wait(
            barrier, reach(1) + 2 * (CHIPS - 1) * is_slow.astype(jnp.int32) + (early <= 1).astype(jnp.int32)
        )

    def send_left(d):
        for way in range(2):

            @pl.when((core == 0) & (d == way) & (position(way) > SLOW))
            def _():
                for chip in range(CHIPS):
                    pair = pl.ds(2 * chip, 2)
                    remote(
                        lefts[way].at[0, pair], even_left.at[way, pair], left_sem.at[way], even_left_got.at[way, chip],
                        layer - sign(way), odd_plane,
                    ).start()

    def send_right(d):
        @pl.when(core == 0)
        def _():
            remote(kept.at[d], even_right.at[d], kept_sem.at[d], even_right_got.at[d], layer, odd_plane).start()

        @pl.when(is_odd & (position(d) >= SLOW) & (position(d) < LAST))
        def _():
            remote(
                kept.at[d], odd_right.at[d], kept_sem.at[d], odd_right_got.at[d], layer + sign(d), odd_plane
            ).start()

    def sent_factors(d):
        @pl.when((core == 0) & (position(d) > SLOW))
        def _():
            remote(even_left.at[d], even_left.at[d], left_sem.at[d], even_left_got.at[d, 0], layer, odd_plane).wait_send()

        @pl.when((core == 0) | ((position(d) >= SLOW) & (position(d) < LAST)))
        def _():
            remote(kept.at[d], even_right.at[d], kept_sem.at[d], even_right_got.at[d], layer, odd_plane).wait_send()

    def mask_right(d):
        for j in range(8):
            top = ranks[0, d, 0, j] * pattern[0, d, 0, j]
            rows = lax.broadcasted_iota(jnp.int32, (128, 1024), 0)
            kept[d, j] = jnp.where(rows < top, kept[d, j].astype(F32), 0.0).astype(BF16)

    send_left(first)
    each(first, lambda way: load_right(way).wait())
    mask_right(first)
    send_right(first)
    each(second, lambda way: load_right(way).start())

    @pl.when(is_odd)
    def _():
        each(second, lambda way: load_left(way).start())

    load_tri.wait()
    load_src.wait()
    row = lax.broadcasted_iota(jnp.int32, (128, 128), 0)
    col = lax.broadcasted_iota(jnp.int32, (128, 128), 1)

    def exact(a, b):
        return jnp.dot(a, b, preferred_element_type=F32, precision=lax.Precision.HIGHEST)

    by_col, units, inverses = [], [], []
    for b in range(8):
        block = tri[b]
        diagonal = jnp.where(row == col, block, 0.0)
        by_row = 1.0 / jnp.sum(diagonal, axis=1, keepdims=True)
        by_col.append(1.0 / jnp.sum(diagonal, axis=0, keepdims=True))
        units.append(jnp.where(row > col, block * by_row, 0.0))
        inverses.append(jnp.where(row == col, 1.0, 0.0))
    for half in (1, 2, 4, 8, 16, 32, 64):
        joins = (row // (2 * half) == col // (2 * half)) & (row // half != col // half)
        for b in range(8):
            part = jnp.where(joins, units[b], 0.0)
            if half > 1:
                part = exact(inverses[b], exact(part, inverses[b]))
            inverses[b] = inverses[b] - part
    for b in range(8):
        solved[:, 128 * b : 128 * (b + 1)] = lax.dot_general(
            src[:, 128 * b : 128 * (b + 1)] * by_col[b], inverses[b], NT,
            preferred_element_type=F32, precision=lax.Precision.HIGHEST,
        )
    sent_solved = solved_odd.at[2]
    sent_solved[...] = solved[...].astype(BF16)
    even_solved = remote(sent_solved, solved_even, solved_sem.at[0], solved_even_got, layer, odd_plane)

    def odd_solved(d):
        return remote(
            sent_solved, solved_odd.at[d], solved_sem.at[d], solved_odd_got.at[d], layer + sign(d), odd_plane
        )

    def sends_solved(d):
        return is_odd & (position(d) < LAST) & ((position(d) == 0) | (position(d) >= SLOW))

    def slow_even(source):
        return remote(source, solved_even, slow_sem.at[0], solved_even_got, layer + forward, 2 * y)

    def slow_odd(source):
        return remote(
            source, solved_odd.at[first], slow_sem.at[1], solved_odd_got.at[first], layer + forward, odd_plane
        )

    @pl.when((core == 0) & (early == 0))
    def _():
        slow_even(sent_solved).start()

    @pl.when(core == 0)
    def _():
        even_solved.start()

    for d in range(2):

        @pl.when(sends_solved(d))
        def _():
            odd_solved(d).start()

    each(second, lambda way: load_right(way).wait())
    mask_right(second)

    def send_second():
        sent_factors(first)
        send_left(second)
        send_right(second)

    def open_way(d):
        each(d, lambda way: load_left(way).wait())

        @pl.when(position(d) >= 1)
        def _():
            remote(sent_solved, solved_odd.at[d], solved_sem.at[d], solved_odd_got.at[d], layer, odd_plane).wait_recv()
            begin = lax.dot_general(
                solved_odd[d], odd_left[d].reshape(1024, 1024), NT, preferred_element_type=F32
            )
            for chip in range(CHIPS):
                odd_start[d, chip] = begin[:, 256 * chip : 256 * (chip + 1)]

    def wait_even_right(d):
        remote(kept.at[d], even_right.at[d], kept_sem.at[d], even_right_got.at[d], layer, odd_plane).wait_recv()

    def make(right, left, d, chip, step):
        block = left[d, pl.ds(2 * chip, 2)].reshape(256, 1024)
        full = right[d].reshape(1024, 1024)
        columns = lax.dot_general(full, block, NT, preferred_element_type=F32).astype(BF16)
        step[d, chip] = columns.reshape(CHIPS, 256, 256)

    def make_odd(d):
        @pl.when(position(d) > SLOW)
        def _():
            remote(kept.at[d], odd_right.at[d], kept_sem.at[d], odd_right_got.at[d], layer, odd_plane).wait_recv()

            @pl.loop(0, CHIPS)
            def _(chip):
                make(odd_right, odd_left, d, chip, odd_step)

    def make_even(d):
        @pl.when((position(d) >= SLOW) & (position(d) < LAST))
        def _():
            @pl.loop(0, CHIPS)
            def _(chip):
                part = even_left.at[d, pl.ds(2 * chip, 2)]
                remote(part, part, left_sem.at[d], even_left_got.at[d, chip], layer, odd_plane).wait_recv()
                block = even_left[d, pl.ds(2 * chip, 2)].reshape(256, 1024)
                even_start[d, chip] = lax.dot_general(solved_even[...], block, NT, preferred_element_type=F32)
                make(even_right, even_left, d, chip, even_step)

    def wait_pieces(ref, got, count):
        remote(ref.at[pl.ds(0, count)], ref.at[pl.ds(0, count)], sent_sem.at[0], got, layer, odd_plane).wait_recv()

    def pair_row(ref, chip):
        return jnp.concatenate([ref[2 * chip], ref[2 * chip + 1]], axis=1)

    def start_only(d, start, deliver):
        for turn in (2, 1, 3, 0):
            other = lax.rem(y + turn, CHIPS)
            deliver(turn, other, start[d, other].astype(BF16))

    def advance(d, ref, got, near, step, start, deliver):
        turns = (2, 1, 3, 0)
        others = {turn: lax.rem(y + turn, CHIPS) for turn in turns}
        wait_pieces(ref, got.at[d, 0], near)
        totals = {turn: start[d, others[turn]] for turn in turns}
        for source in (0, 1, 3):
            values = pair_row(ref, others[source])
            for turn in turns:
                totals[turn] += jnp.dot(
                    values, step[d, others[turn], others[source]], preferred_element_type=F32
                )
        wait_pieces(ref, got.at[d, 1], 2)
        values = pair_row(ref, others[2])
        for turn in turns:
            total = totals[turn] + jnp.dot(values, step[d, others[turn], others[2]], preferred_element_type=F32)
            deliver(turn, others[turn], total.astype(BF16))

    def far(turn):
        return 1 if turn == 2 else 0

    def odd_deliver(d):
        q = position(d)
        direct = (q == LAST) | (q < SLOW)

        def deliver(turn, other, result):
            for part in range(2):
                sent[d, 1, other, part] = result[:, 128 * part : 128 * (part + 1)]
            if turn == 0:
                even_in[d, odd_plane] = result[:, :128]
            else:
                remote(
                    sent.at[d, 1, other, 0], even_in.at[d, odd_plane], sent_sem.at[d], even_in_got.at[d, far(turn)],
                    layer, 2 * other + 1,
                ).start()

            @pl.when(jnp.logical_not(direct))
            def _():
                remote(
                    sent.at[d, 1, other, 1], odd_in.at[d, odd_plane], sent_sem.at[d], odd_in_got.at[d, far(turn)],
                    layer + sign(d), 2 * other + 1,
                ).start()

            @pl.when(direct)
            def _():
                if turn == 0:
                    own_in[d, odd_plane] = result[:, 128:]
                else:
                    remote(
                        sent.at[d, 1, other, 1], own_in.at[d, odd_plane], sent_sem.at[d], own_in_got.at[d],
                        layer, 2 * other + 1,
                    ).start()

        return deliver

    def run_odd(d):
        @pl.when(position(d) > SLOW)
        def _():
            advance(d, odd_in.at[d], odd_in_got, 6, odd_step, odd_start, odd_deliver(d))

    def run_even(d):
        q = position(d)

        def deliver(turn, other, result):
            for part in range(2):
                sent[d, 0, other, part] = result[:, 128 * part : 128 * (part + 1)]
            remote(
                sent.at[d, 0, other, 0], even_in.at[d, 2 * y], sent_sem.at[d], even_in_got.at[d, far(turn)],
                layer + sign(d), 2 * other + 1,
            ).start()

            @pl.when(q < LAST - 1)
            def _():
                remote(
                    sent.at[d, 0, other, 1], odd_in.at[d, 2 * y], sent_sem.at[d], odd_in_got.at[d, far(turn)],
                    layer + 2 * sign(d), 2 * other + 1,
                ).start()

            @pl.when(q == LAST - 1)
            def _():
                remote(
                    sent.at[d, 0, other, 1], own_in.at[d, 2 * y], sent_sem.at[d], own_in_got.at[d],
                    layer + sign(d), 2 * other + 1,
                ).start()

        @pl.when((q >= SLOW) & (q < LAST))
        def _():
            advance(d, even_in.at[d], even_in_got, 5, even_step, even_start, deliver)

        @pl.when(q == LAST)
        def _():
            wait_pieces(even_in.at[d], even_in_got.at[d, 0], 5)
            wait_pieces(even_in.at[d], even_in_got.at[d, 1], 2)

    def slow_deliver(turn, other, result):
        for part in range(2):
            sent[first, 0, other, part] = result[:, 128 * part : 128 * (part + 1)]
        remote(
            sent.at[first, 0, other, 0], even_in.at[first, 2 * y], sent_sem.at[first],
            even_in_got.at[first, far(turn)], layer, 2 * other + 1,
        ).start()

        @pl.when(early < SLOW)
        def _():
            remote(
                sent.at[first, 0, other, 1], own_in.at[first, 2 * y], sent_sem.at[first], own_in_got.at[first],
                layer, 2 * other + 1,
            ).start()

        @pl.when(early == SLOW)
        def _():
            remote(
                sent.at[first, 0, other, 1], odd_in.at[first, 2 * y], sent_sem.at[first],
                odd_in_got.at[first, far(turn)], layer + forward, 2 * other + 1,
            ).start()

    @pl.when((core == 0) & is_slow)
    def _():
        each(first, lambda way: load_left(way).wait())
        remote(sent_solved, solved_even, solved_sem.at[0], solved_even_got, layer, 2 * y).wait_recv()
        for turn in (2, 1, 3, 0):
            other = lax.rem(y + turn, CHIPS)
            block = odd_left[first, pl.ds(2 * other, 2)].reshape(256, 1024)
            result = lax.dot_general(solved_even[...], block, NT, preferred_element_type=F32)
            slow_deliver(turn, other, result.astype(BF16))

    def slow_step():
        wait_pieces(even_in.at[first], even_in_got.at[first, 0], 5)
        wait_pieces(even_in.at[first], even_in_got.at[first, 1], 2)
        trace = jnp.dot(
            piece_row(even_in.at[first]), even_right[first].reshape(1024, 1024), preferred_element_type=F32
        )
        slow_sent[0] = (solved_even[...].astype(F32) + trace).astype(BF16)
        slow_even(slow_sent.at[0]).start()
        wait_pieces(own_in.at[first], own_in_got.at[first], 7)
        trace = jnp.dot(
            piece_row(own_in.at[first]), kept[first].reshape(1024, 1024), preferred_element_type=F32
        )
        slow_sent[1] = (solved[...] + trace).astype(BF16)
        slow_odd(slow_sent.at[1]).start()

    def relay_even(d):
        return remote(even_in.at[d], own_in.at[d], relay_sem.at[0, d], own_in_got.at[d], layer, 2 * y)

    def relay_odd(d):
        return remote(odd_in.at[d], own_in.at[d], relay_sem.at[1, d], own_in_got.at[d], layer - sign(d), odd_plane)

    def sweep(d):
        q = position(d)
        run_even(d)

        @pl.when(q >= 1)
        def _():
            relay_even(d).start()

        @pl.when(q > SLOW)
        def _():
            relay_odd(d).start()

    @pl.when(is_odd)
    def _():
        remote(sent_solved, solved_even, solved_sem.at[0], solved_even_got, layer, odd_plane).wait_recv()
        wait_even_right(first)
        open_way(first)

        @pl.when(is_slow)
        def _():
            start_only(first, odd_start, odd_deliver(first))

        @pl.when((early >= 1) & (early < SLOW))
        def _():
            slow_step()

        @pl.when(position(first) >= SEND_EARLY)
        def _():
            send_second()

        make_odd(first)

        @pl.when(early <= SLOW + 1)
        def _():
            run_odd(first)

        make_even(first)

        @pl.when(position(first) >= MAKE_EARLY)
        def _():
            wait_even_right(second)
            open_way(second)
            make_odd(second)
            make_even(second)

        @pl.when(early > SLOW + 1)
        def _():
            run_odd(first)

        sweep(first)

        @pl.when(position(first) < SEND_EARLY)
        def _():
            pl.semaphore_signal(go_sem, inc=1, device_id=(layer, 2 * y), device_id_type=MESH)
            send_second()

        @pl.when(position(first) < MAKE_EARLY)
        def _():
            wait_even_right(second)
            open_way(second)
            make_odd(second)
            make_even(second)

        run_odd(second)
        sweep(second)

    @pl.when(core == 0)
    def _():
        @pl.when(position(first) < SEND_EARLY)
        def _():
            pl.semaphore_wait(go_sem, 1)

        send_second()

    def add_own(d):
        q = position(d)

        @pl.when(q >= 1)
        def _():
            @pl.when(is_odd & (q == LAST))
            def _():
                wait_pieces(own_in.at[d], own_in_got.at[d], 7)

            @pl.when((core == 0) | ((q >= SLOW) & (q < LAST)))
            def _():
                wait_pieces(own_in.at[d], own_in_got.at[d], 8)

            solved[...] += jnp.dot(
                piece_row(own_in.at[d]), kept[d].reshape(1024, 1024), preferred_element_type=F32
            )

    add_own(first)
    add_own(second)
    out[0] = solved[...]

    sent_factors(second)

    def drain(d, count):
        part = odd_in.at[d, pl.ds(0, count)]
        remote(part, part, sent_sem.at[d], own_in_got.at[d], layer, odd_plane).wait_send()

    @pl.when(core == 0)
    def _():
        even_solved.wait_send()

        @pl.when(early == 0)
        def _():
            slow_even(sent_solved).wait_send()

        @pl.when(is_slow)
        def _():
            drain(first, 8)

    @pl.when(is_odd)
    def _():
        @pl.when((early >= 1) & (early < SLOW))
        def _():
            slow_even(slow_sent.at[0]).wait_send()
            slow_odd(slow_sent.at[1]).wait_send()

        for d in range(2):
            q = position(d)

            @pl.when(sends_solved(d))
            def _():
                odd_solved(d).wait_send()

            @pl.when((q >= SLOW) & (q < LAST))
            def _():
                drain(d, 8)

            @pl.when((q >= SLOW) & (q < LAST))
            def _():
                drain(d, 7)

            @pl.when((q == LAST) | ((q >= 1) & (q < SLOW)))
            def _():
                drain(d, 6)

            @pl.when(q >= 1)
            def _():
                relay_even(d).wait_send()

            @pl.when(q > SLOW)
            def _():
                relay_odd(d).wait_send()


def shards(*arrays):
    anywhere = pl.BlockSpec(memory_space=pl.ANY)
    scalars = pl.BlockSpec(memory_space=pltpu.SMEM)
    dma, vmem = pltpu.SemaphoreType.DMA, pltpu.VMEM
    return pl.pallas_call(
        kernel,
        name="sweep",
        out_shape=jax.ShapeDtypeStruct((1, SOURCES, 1024), F32),
        in_specs=[anywhere] * 6 + [scalars] * 2,
        out_specs=pl.BlockSpec(memory_space=pltpu.VMEM),
        scratch_shapes=[
            vmem((SOURCES, 1024), F32),
            vmem((8, 128, 128), F32),
            vmem((SOURCES, 1024), F32),
            vmem((SOURCES, 1024), BF16),
            vmem((3, SOURCES, 1024), BF16),
            vmem((2, 8, 128, 1024), BF16),
            vmem((2, 8, 128, 1024), BF16),
            vmem((2, 8, 128, 1024), BF16),
            vmem((2, 8, 128, 1024), BF16),
            vmem((2, 8, 128, 1024), BF16),
            vmem((2, CHIPS, CHIPS, 256, 256), BF16),
            vmem((2, CHIPS, CHIPS, 256, 256), BF16),
            vmem((2, CHIPS, SOURCES, 256), F32),
            vmem((2, CHIPS, SOURCES, 256), F32),
            vmem((2, 8, SOURCES, 128), BF16),
            vmem((2, 8, SOURCES, 128), BF16),
            vmem((2, 8, SOURCES, 128), BF16),
            vmem((2, 2, CHIPS, 2, SOURCES, 128), BF16),
            vmem((2, SOURCES, 1024), BF16),
            dma((6,)),
            dma((2,)),
            dma((2,)),
            dma((2,)),
            dma((2,)),
            dma((2, 2)),
            dma((2,)),
            dma((2,)),
            dma((2,)),
            dma((2, CHIPS)),
            dma(()),
            dma((2,)),
            dma((2, 2)),
            dma((2, 2)),
            dma((2,)),
            pltpu.SemaphoreType.REGULAR,
        ],
        compiler_params=pltpu.CompilerParams(
            collective_id=0, has_side_effects=True, vmem_limit_bytes=56 << 20
        ),
    )(*arrays)


def solution(mesh):
    in_specs = (
        P("layer", None, "plane"),
        P("layer", "plane", None, None),
        P("layer", None, None, "plane"),
        P("layer", None, None, "plane"),
        P("layer", None, None, "plane"),
        P("layer", None, None, "plane"),
        P("layer", None, "plane", None),
        P("layer", None, "plane", None),
    )
    return jax.shard_map(
        shards, mesh=mesh, in_specs=in_specs, out_specs=P("layer", None, "plane"), check_vma=False
    )
```

time: 158 us -> 145 us (0.918)
  Pallas kernels: 156 us -> 144 us
    pallas_call x1, Pallas kernels: 156 us -> 144 us  [shards(): pl.pallas_call(kernel, name='sweep', out_shape=jax.ShapeDtypeStruct((1, S...]
where the time goes in v2:
time: 145 us
  Pallas kernels  144 us (99%)
  local copies, waits for them, and re-layouts  1.47 us (1%)
    pallas_call x1, Pallas kernels, shards(): pl.pallas_call(kernel, name='sweep', out_shape=jax.ShapeDtypeStruct((1, S...  144 us

profile of v2, /device:TPU:1, one launch (start us, length us, event | category | flops | bytes accessed | tf_op | source)
XLA Modules:
  0.0 145.1 jit_solution(1339016580996628851)
XLA Ops:
  0.0 143.6 %sweep.1 = f32[1,16,1024]{2,1,0:T(8,128)} custom-call(f32[1,16,1024]{2,1,0:T(8,128)} %sources.1, f32[1,8,128,128]{3,2,1,0:T(8,128)} %fronts.1, bf16[1,8,128,1024]{3,2,1,0:T(8,128)(2,1)} %down_left.1, bf16[1,8,128,1024]{3,2,1,0:T(8,128)(2,1)} %down_right.1, bf16[1,8,128,1024]{3,2,1,0:T(8,128)(2,1)} %up_left.1, bf16[1,8,128,1024]{3,2,1,0:T(8,128)(2,1)} %up_right.1, ...), custom_call_target="tpu_custom_call" | custom-call | tf_op jit(solution)/shard_map/sweep/pallas_call | solution.py:604
  143.6 1.5 %copy.10 = f32[1,16,1024]{2,1,0:T(8,128)} copy(f32[1,16,1024]{2,1,0:T(8,128)} %sweep.1) | data formatting | bytes 131072

commit v3 on v2

--- a/solution.py
+++ b/solution.py
@@ -21,9 +21,9 @@
 def kernel(
     sources, fronts, down_left, down_right, up_left, up_right, ranks, pattern, out,
     src, tri, solved, solved_even, solved_odd, kept, even_right, odd_right, even_left, odd_left,
-    even_step, odd_step, even_start, odd_start, even_in, odd_in, own_in, sent,
+    even_step, odd_step, even_start, odd_start, even_in, pieces, sent,
     slow_sent, load_sem, kept_sem, left_sem, solved_sem, sent_sem, relay_sem, slow_sem,
-    even_right_got, odd_right_got, even_left_got, solved_even_got, solved_odd_got, even_in_got, odd_in_got, own_in_got, go_sem,
+    even_right_got, odd_right_got, even_left_got, solved_even_got, solved_odd_got, even_in_got, got, go_sem,
 ):
     layer, plane = lax.axis_index("layer"), lax.axis_index("plane")
     y, core = plane // 2, lax.rem(plane, 2)
@@ -272,22 +272,28 @@
         columns = lax.dot_general(full, block, NT, preferred_element_type=F32).astype(BF16)
         step[d, chip] = columns.reshape(CHIPS, 256, 256)
 
+    def wait_odd_right(d):
+        remote(kept.at[d], odd_right.at[d], kept_sem.at[d], odd_right_got.at[d], layer, odd_plane).wait_recv()
+
     def make_odd(d):
         @pl.when(position(d) > SLOW)
         def _():
-            remote(kept.at[d], odd_right.at[d], kept_sem.at[d], odd_right_got.at[d], layer, odd_plane).wait_recv()
+            wait_odd_right(d)
 
             @pl.loop(0, CHIPS)
             def _(chip):
                 make(odd_right, odd_left, d, chip, odd_step)
 
+    def wait_even_left(d, chip):
+        part = even_left.at[d, pl.ds(2 * chip, 2)]
+        remote(part, part, left_sem.at[d], even_left_got.at[d, chip], layer, odd_plane).wait_recv()
+
     def make_even(d):
-        @pl.when((position(d) >= SLOW) & (position(d) < LAST))
+        @pl.when((position(d) > SLOW + 1) & (position(d) < LAST))
         def _():
             @pl.loop(0, CHIPS)
             def _(chip):
-                part = even_left.at[d, pl.ds(2 * chip, 2)]
-                remote(part, part, left_sem.at[d], even_left_got.at[d, chip], layer, odd_plane).wait_recv()
+                wait_even_left(d, chip)
                 block = even_left[d, pl.ds(2 * chip, 2)].reshape(256, 1024)
                 even_start[d, chip] = lax.dot_general(solved_even[...], block, NT, preferred_element_type=F32)
                 make(even_right, even_left, d, chip, even_step)
@@ -303,10 +309,10 @@
             other = lax.rem(y + turn, CHIPS)
             deliver(turn, other, start[d, other].astype(BF16))
 
-    def advance(d, ref, got, near, step, start, deliver):
+    def advance(d, ref, got_near, got_far, near, step, start, deliver):
         turns = (2, 1, 3, 0)
         others = {turn: lax.rem(y + turn, CHIPS) for turn in turns}
-        wait_pieces(ref, got.at[d, 0], near)
+        wait_pieces(ref, got_near, near)
         totals = {turn: start[d, others[turn]] for turn in turns}
         for source in (0, 1, 3):
             values = pair_row(ref, others[source])
@@ -314,7 +320,7 @@
                 totals[turn] += jnp.dot(
                     values, step[d, others[turn], others[source]], preferred_element_type=F32
                 )
-        wait_pieces(ref, got.at[d, 1], 2)
+        wait_pieces(ref, got_far, 2)
         values = pair_row(ref, others[2])
         for turn in turns:
             total = totals[turn] + jnp.dot(values, step[d, others[turn], others[2]], preferred_element_type=F32)
@@ -326,6 +332,8 @@
     def odd_deliver(d):
         q = position(d)
         direct = (q == LAST) | (q < SLOW)
+        kind = direct.astype(jnp.int32)
+        odd_layer = layer + (1 - kind) * sign(d)
 
         def deliver(turn, other, result):
             for part in range(2):
@@ -338,32 +346,28 @@
                     layer, 2 * other + 1,
                 ).start()
 
-            @pl.when(jnp.logical_not(direct))
-            def _():
-                remote(
-                    sent.at[d, 1, other, 1], odd_in.at[d, odd_plane], sent_sem.at[d], odd_in_got.at[d, far(turn)],
-                    layer + sign(d), 2 * other + 1,
-                ).start()
-
-            @pl.when(direct)
-            def _():
-                if turn == 0:
-                    own_in[d, odd_plane] = result[:, 128:]
-                else:
-                    remote(
-                        sent.at[d, 1, other, 1], own_in.at[d, odd_plane], sent_sem.at[d], own_in_got.at[d],
-                        layer, 2 * other + 1,
-                    ).start()
+            odd_part = remote(
+                sent.at[d, 1, other, 1], pieces.at[kind, d, odd_plane], sent_sem.at[d], got.at[kind, d, far(turn)],
+                odd_layer, 2 * other + 1,
+            )
+            if turn != 0:
+                odd_part.start()
+            else:
+                pl.when(jnp.logical_not(direct))(odd_part.start)
+
+                @pl.when(direct)
+                def _():
+                    pieces[1, d, odd_plane] = result[:, 128:]
 
         return deliver
 
     def run_odd(d):
         @pl.when(position(d) > SLOW)
         def _():
-            advance(d, odd_in.at[d], odd_in_got, 6, odd_step, odd_start, odd_deliver(d))
-
-    def run_even(d):
-        q = position(d)
+            advance(d, pieces.at[0, d], got.at[0, d, 0], got.at[0, d, 1], 6, odd_step, odd_start, odd_deliver(d))
+
+    def even_deliver(d):
+        kind = (position(d) == LAST - 1).astype(jnp.int32)
 
         def deliver(turn, other, result):
             for part in range(2):
@@ -373,23 +377,22 @@
                 layer + sign(d), 2 * other + 1,
             ).start()
 
-            @pl.when(q < LAST - 1)
-            def _():
-                remote(
-                    sent.at[d, 0, other, 1], odd_in.at[d, 2 * y], sent_sem.at[d], odd_in_got.at[d, far(turn)],
-                    layer + 2 * sign(d), 2 * other + 1,
-                ).start()
-
-            @pl.when(q == LAST - 1)
-            def _():
-                remote(
-                    sent.at[d, 0, other, 1], own_in.at[d, 2 * y], sent_sem.at[d], own_in_got.at[d],
-                    layer + sign(d), 2 * other + 1,
-                ).start()
-
-        @pl.when((q >= SLOW) & (q < LAST))
-        def _():
-            advance(d, even_in.at[d], even_in_got, 5, even_step, even_start, deliver)
+            remote(
+                sent.at[d, 0, other, 1], pieces.at[kind, d, 2 * y], sent_sem.at[d], got.at[kind, d, far(turn)],
+                layer + (2 - kind) * sign(d), 2 * other + 1,
+            ).start()
+
+        return deliver
+
+    def run_even(d):
+        q = position(d)
+
+        @pl.when((q > SLOW + 1) & (q < LAST))
+        def _():
+            advance(
+                d, even_in.at[d], even_in_got.at[d, 0], even_in_got.at[d, 1], 5, even_step, even_start,
+                even_deliver(d),
+            )
 
         @pl.when(q == LAST)
         def _():
@@ -404,19 +407,11 @@
             even_in_got.at[first, far(turn)], layer, 2 * other + 1,
         ).start()
 
-        @pl.when(early < SLOW)
-        def _():
-            remote(
-                sent.at[first, 0, other, 1], own_in.at[first, 2 * y], sent_sem.at[first], own_in_got.at[first],
-                layer, 2 * other + 1,
-            ).start()
-
-        @pl.when(early == SLOW)
-        def _():
-            remote(
-                sent.at[first, 0, other, 1], odd_in.at[first, 2 * y], sent_sem.at[first],
-                odd_in_got.at[first, far(turn)], layer + forward, 2 * other + 1,
-            ).start()
+        kind = (early < SLOW).astype(jnp.int32)
+        remote(
+            sent.at[first, 0, other, 1], pieces.at[kind, first, 2 * y], sent_sem.at[first],
+            got.at[kind, first, far(turn)], layer + (1 - kind) * forward, 2 * other + 1,
+        ).start()
 
     @pl.when((core == 0) & is_slow)
     def _():
@@ -427,6 +422,27 @@
             block = odd_left[first, pl.ds(2 * other, 2)].reshape(256, 1024)
             result = lax.dot_general(solved_even[...], block, NT, preferred_element_type=F32)
             slow_deliver(turn, other, result.astype(BF16))
+
+    def join(ref, right, left, part, deliver):
+        trace = jnp.dot(piece_row(ref), right[first].reshape(1024, 1024), preferred_element_type=F32)
+        whole = (part.astype(F32) + trace).astype(BF16)
+        for turn in (2, 1, 3, 0):
+            other = lax.rem(y + turn, CHIPS)
+            block = left[first, pl.ds(2 * other, 2)].reshape(256, 1024)
+            deliver(turn, other, lax.dot_general(whole, block, NT, preferred_element_type=F32).astype(BF16))
+
+    def join_odd():
+        wait_odd_right(first)
+        wait_pieces(pieces.at[0, first], got.at[0, first, 0], 6)
+        wait_pieces(pieces.at[0, first], got.at[0, first, 1], 2)
+        join(pieces.at[0, first], odd_right, odd_left, solved_odd[first], odd_deliver(first))
+
+    def join_even():
+        for chip in range(CHIPS):
+            wait_even_left(first, chip)
+        wait_pieces(even_in.at[first], even_in_got.at[first, 0], 5)
+        wait_pieces(even_in.at[first], even_in_got.at[first, 1], 2)
+        join(even_in.at[first], even_right, even_left, solved_even[...], even_deliver(first))
 
     def slow_step():
         wait_pieces(even_in.at[first], even_in_got.at[first, 0], 5)
@@ -436,18 +452,19 @@
         )
         slow_sent[0] = (solved_even[...].astype(F32) + trace).astype(BF16)
         slow_even(slow_sent.at[0]).start()
-        wait_pieces(own_in.at[first], own_in_got.at[first], 7)
+        wait_pieces(pieces.at[1, first], got.at[1, first, 0], 5)
+        wait_pieces(pieces.at[1, first], got.at[1, first, 1], 2)
         trace = jnp.dot(
-            piece_row(own_in.at[first]), kept[first].reshape(1024, 1024), preferred_element_type=F32
+            piece_row(pieces.at[1, first]), kept[first].reshape(1024, 1024), preferred_element_type=F32
         )
         slow_sent[1] = (solved[...] + trace).astype(BF16)
         slow_odd(slow_sent.at[1]).start()
 
     def relay_even(d):
-        return remote(even_in.at[d], own_in.at[d], relay_sem.at[0, d], own_in_got.at[d], layer, 2 * y)
+        return remote(even_in.at[d], pieces.at[1, d], relay_sem.at[0, d], got.at[1, d, 0], layer, 2 * y)
 
     def relay_odd(d):
-        return remote(odd_in.at[d], own_in.at[d], relay_sem.at[1, d], own_in_got.at[d], layer - sign(d), odd_plane)
+        return remote(pieces.at[0, d], pieces.at[1, d], relay_sem.at[1, d], got.at[1, d, 0], layer - sign(d), odd_plane)
 
     def sweep(d):
         q = position(d)
@@ -479,11 +496,17 @@
         def _():
             send_second()
 
-        make_odd(first)
-
-        @pl.when(early <= SLOW + 1)
-        def _():
-            run_odd(first)
+        @pl.when(early == SLOW + 1)
+        def _():
+            join_odd()
+
+        @pl.when((early == SLOW) | (early == SLOW + 1))
+        def _():
+            join_even()
+
+        @pl.when(early > SLOW + 1)
+        def _():
+            make_odd(first)
 
         make_even(first)
 
@@ -530,14 +553,15 @@
         def _():
             @pl.when(is_odd & (q == LAST))
             def _():
-                wait_pieces(own_in.at[d], own_in_got.at[d], 7)
+                wait_pieces(pieces.at[1, d], got.at[1, d, 0], 5)
+                wait_pieces(pieces.at[1, d], got.at[1, d, 1], 2)
 
             @pl.when((core == 0) | ((q >= SLOW) & (q < LAST)))
             def _():
-                wait_pieces(own_in.at[d], own_in_got.at[d], 8)
+                wait_pieces(pieces.at[1, d], got.at[1, d, 0], 8)
 
             solved[...] += jnp.dot(
-                piece_row(own_in.at[d]), kept[d].reshape(1024, 1024), preferred_element_type=F32
+                piece_row(pieces.at[1, d]), kept[d].reshape(1024, 1024), preferred_element_type=F32
             )
 
     add_own(first)
@@ -547,8 +571,8 @@
     sent_factors(second)
 
     def drain(d, count):
-        part = odd_in.at[d, pl.ds(0, count)]
-        remote(part, part, sent_sem.at[d], own_in_got.at[d], layer, odd_plane).wait_send()
+        part = pieces.at[0, d, pl.ds(0, count)]
+        remote(part, part, sent_sem.at[d], got.at[1, d, 0], layer, odd_plane).wait_send()
 
     @pl.when(core == 0)
     def _():
@@ -623,8 +647,7 @@
             vmem((2, CHIPS, SOURCES, 256), F32),
             vmem((2, CHIPS, SOURCES, 256), F32),
             vmem((2, 8, SOURCES, 128), BF16),
-            vmem((2, 8, SOURCES, 128), BF16),
-            vmem((2, 8, SOURCES, 128), BF16),
+            vmem((2, 2, 8, SOURCES, 128), BF16),
             vmem((2, 2, CHIPS, 2, SOURCES, 128), BF16),
             vmem((2, SOURCES, 1024), BF16),
             dma((6,)),
@@ -640,8 +663,7 @@
             dma(()),
             dma((2,)),
             dma((2, 2)),
-            dma((2, 2)),
-            dma((2,)),
+            dma((2, 2, 2)),
             pltpu.SemaphoreType.REGULAR,
         ],
         compiler_params=pltpu.CompilerParams(

time: 145 us -> 144 us (level)
  Pallas kernels: 144 us -> 142 us
where the time goes in v3:
time: 144 us
  Pallas kernels  142 us (99%)
  local copies, waits for them, and re-layouts  1.47 us (1%)
    pallas_call x1, Pallas kernels, shards(): pl.pallas_call(kernel, name='sweep', out_shape=jax.ShapeDtypeStruct((1, S...  142 us

profile of v3, /device:TPU:1, one launch (start us, length us, event | category | flops | bytes accessed | tf_op | source)
XLA Modules:
  0.0 143.7 jit_solution(12424631817831497673)
XLA Ops:
  0.0 142.3 %sweep.1 = f32[1,16,1024]{2,1,0:T(8,128)} custom-call(f32[1,16,1024]{2,1,0:T(8,128)} %sources.1, f32[1,8,128,128]{3,2,1,0:T(8,128)} %fronts.1, bf16[1,8,128,1024]{3,2,1,0:T(8,128)(2,1)} %down_left.1, bf16[1,8,128,1024]{3,2,1,0:T(8,128)(2,1)} %down_right.1, bf16[1,8,128,1024]{3,2,1,0:T(8,128)(2,1)} %up_left.1, bf16[1,8,128,1024]{3,2,1,0:T(8,128)(2,1)} %up_right.1, ...), custom_call_target="tpu_custom_call" | custom-call | tf_op jit(solution)/shard_map/sweep/pallas_call | solution.py:628
  142.3 1.5 %copy.10 = f32[1,16,1024]{2,1,0:T(8,128)} copy(f32[1,16,1024]{2,1,0:T(8,128)} %sweep.1) | data formatting | bytes 131072

commit v4 on v3

--- a/solution.py
+++ b/solution.py
@@ -309,25 +309,37 @@
             other = lax.rem(y + turn, CHIPS)
             deliver(turn, other, start[d, other].astype(BF16))
 
-    def advance(d, ref, got_near, got_far, near, step, start, deliver):
-        turns = (2, 1, 3, 0)
-        others = {turn: lax.rem(y + turn, CHIPS) for turn in turns}
-        wait_pieces(ref, got_near, near)
-        totals = {turn: start[d, others[turn]] for turn in turns}
-        for source in (0, 1, 3):
-            values = pair_row(ref, others[source])
-            for turn in turns:
-                totals[turn] += jnp.dot(
-                    values, step[d, others[turn], others[source]], preferred_element_type=F32
+    last_y, first_y = (y == CHIPS - 1).astype(jnp.int32), (y == 0).astype(jnp.int32)
+    comes = (0, 1 + 2 * last_y, 3 - last_y, 2 - last_y)
+    goes = (2 + first_y, 1 + first_y, 3 - 2 * first_y, 0)
+
+    def chip_at(turn):
+        return lax.rem(y + turn, CHIPS)
+
+    def seen(turn):
+        return lax.rem(CHIPS - turn, CHIPS)
+
+    def wait_from(ref, got, turn, count):
+        wait_pieces(ref, got.at[turn], count)
+
+    def wait_all(ref, got, own):
+        for turn in range(CHIPS):
+            wait_from(ref, got, turn, own if turn == 0 else 2)
+
+    def advance(d, ref, got, own, step, start, deliver):
+        totals = [start[d, chip_at(turn)] for turn in goes]
+        for at, source in enumerate(comes):
+            if at != 1:
+                wait_from(ref, got, source, own if at == 0 else 2)
+            if at == 0:
+                wait_from(ref, got, comes[1], 2)
+            values = pair_row(ref, chip_at(source))
+            for index, turn in enumerate(goes):
+                totals[index] += jnp.dot(
+                    values, step[d, chip_at(turn), chip_at(source)], preferred_element_type=F32
                 )
-        wait_pieces(ref, got_far, 2)
-        values = pair_row(ref, others[2])
-        for turn in turns:
-            total = totals[turn] + jnp.dot(values, step[d, others[turn], others[2]], preferred_element_type=F32)
-            deliver(turn, others[turn], total.astype(BF16))
-
-    def far(turn):
-        return 1 if turn == 2 else 0
+                if at == CHIPS - 1:
+                    deliver(turn, chip_at(turn), totals[index].astype(BF16))
 
     def odd_deliver(d):
         q = position(d)
@@ -338,19 +350,19 @@
         def deliver(turn, other, result):
             for part in range(2):
                 sent[d, 1, other, part] = result[:, 128 * part : 128 * (part + 1)]
-            if turn == 0:
+            if isinstance(turn, int) and turn == 0:
                 even_in[d, odd_plane] = result[:, :128]
             else:
                 remote(
-                    sent.at[d, 1, other, 0], even_in.at[d, odd_plane], sent_sem.at[d], even_in_got.at[d, far(turn)],
+                    sent.at[d, 1, other, 0], even_in.at[d, odd_plane], sent_sem.at[d], even_in_got.at[d, seen(turn)],
                     layer, 2 * other + 1,
                 ).start()
 
             odd_part = remote(
-                sent.at[d, 1, other, 1], pieces.at[kind, d, odd_plane], sent_sem.at[d], got.at[kind, d, far(turn)],
+                sent.at[d, 1, other, 1], pieces.at[kind, d, odd_plane], sent_sem.at[d], got.at[kind, d, seen(turn)],
                 odd_layer, 2 * other + 1,
             )
-            if turn != 0:
+            if not isinstance(turn, int) or turn != 0:
                 odd_part.start()
             else:
                 pl.when(jnp.logical_not(direct))(odd_part.start)
@@ -364,7 +376,7 @@
     def run_odd(d):
         @pl.when(position(d) > SLOW)
         def _():
-            advance(d, pieces.at[0, d], got.at[0, d, 0], got.at[0, d, 1], 6, odd_step, odd_start, odd_deliver(d))
+            advance(d, pieces.at[0, d], got.at[0, d], 2, odd_step, odd_start, odd_deliver(d))
 
     def even_deliver(d):
         kind = (position(d) == LAST - 1).astype(jnp.int32)
@@ -373,12 +385,12 @@
             for part in range(2):
                 sent[d, 0, other, part] = result[:, 128 * part : 128 * (part + 1)]
             remote(
-                sent.at[d, 0, other, 0], even_in.at[d, 2 * y], sent_sem.at[d], even_in_got.at[d, far(turn)],
+                sent.at[d, 0, other, 0], even_in.at[d, 2 * y], sent_sem.at[d], even_in_got.at[d, seen(turn)],
                 layer + sign(d), 2 * other + 1,
             ).start()
 
             remote(
-                sent.at[d, 0, other, 1], pieces.at[kind, d, 2 * y], sent_sem.at[d], got.at[kind, d, far(turn)],
+                sent.at[d, 0, other, 1], pieces.at[kind, d, 2 * y], sent_sem.at[d], got.at[kind, d, seen(turn)],
                 layer + (2 - kind) * sign(d), 2 * other + 1,
             ).start()
 
@@ -390,27 +402,26 @@
         @pl.when((q > SLOW + 1) & (q < LAST))
         def _():
             advance(
-                d, even_in.at[d], even_in_got.at[d, 0], even_in_got.at[d, 1], 5, even_step, even_start,
+                d, even_in.at[d], even_in_got.at[d], 1, even_step, even_start,
                 even_deliver(d),
             )
 
         @pl.when(q == LAST)
         def _():
-            wait_pieces(even_in.at[d], even_in_got.at[d, 0], 5)
-            wait_pieces(even_in.at[d], even_in_got.at[d, 1], 2)
+            wait_all(even_in.at[d], even_in_got.at[d], 1)
 
     def slow_deliver(turn, other, result):
         for part in range(2):
             sent[first, 0, other, part] = result[:, 128 * part : 128 * (part + 1)]
         remote(
             sent.at[first, 0, other, 0], even_in.at[first, 2 * y], sent_sem.at[first],
-            even_in_got.at[first, far(turn)], layer, 2 * other + 1,
+            even_in_got.at[first, seen(turn)], layer, 2 * other + 1,
         ).start()
 
         kind = (early < SLOW).astype(jnp.int32)
         remote(
             sent.at[first, 0, other, 1], pieces.at[kind, first, 2 * y], sent_sem.at[first],
-            got.at[kind, first, far(turn)], layer + (1 - kind) * forward, 2 * other + 1,
+            got.at[kind, first, seen(turn)], layer + (1 - kind) * forward, 2 * other + 1,
         ).start()
 
     @pl.when((core == 0) & is_slow)
@@ -433,27 +444,23 @@
 
     def join_odd():
         wait_odd_right(first)
-        wait_pieces(pieces.at[0, first], got.at[0, first, 0], 6)
-        wait_pieces(pieces.at[0, first], got.at[0, first, 1], 2)
+        wait_all(pieces.at[0, first], got.at[0, first], 2)
         join(pieces.at[0, first], odd_right, odd_left, solved_odd[first], odd_deliver(first))
 
     def join_even():
         for chip in range(CHIPS):
             wait_even_left(first, chip)
-        wait_pieces(even_in.at[first], even_in_got.at[first, 0], 5)
-        wait_pieces(even_in.at[first], even_in_got.at[first, 1], 2)
+        wait_all(even_in.at[first], even_in_got.at[first], 1)
         join(even_in.at[first], even_right, even_left, solved_even[...], even_deliver(first))
 
     def slow_step():
-        wait_pieces(even_in.at[first], even_in_got.at[first, 0], 5)
-        wait_pieces(even_in.at[first], even_in_got.at[first, 1], 2)
+        wait_all(even_in.at[first], even_in_got.at[first], 1)
         trace = jnp.dot(
             piece_row(even_in.at[first]), even_right[first].reshape(1024, 1024), preferred_element_type=F32
         )
         slow_sent[0] = (solved_even[...].astype(F32) + trace).astype(BF16)
         slow_even(slow_sent.at[0]).start()
-        wait_pieces(pieces.at[1, first], got.at[1, first, 0], 5)
-        wait_pieces(pieces.at[1, first], got.at[1, first, 1], 2)
+        wait_all(pieces.at[1, first], got.at[1, first], 1)
         trace = jnp.dot(
             piece_row(pieces.at[1, first]), kept[first].reshape(1024, 1024), preferred_element_type=F32
         )
@@ -553,8 +560,7 @@
         def _():
             @pl.when(is_odd & (q == LAST))
             def _():
-                wait_pieces(pieces.at[1, d], got.at[1, d, 0], 5)
-                wait_pieces(pieces.at[1, d], got.at[1, d, 1], 2)
+                wait_all(pieces.at[1, d], got.at[1, d], 1)
 
             @pl.when((core == 0) | ((q >= SLOW) & (q < LAST)))
             def _():
@@ -662,8 +668,8 @@
             dma((2, CHIPS)),
             dma(()),
             dma((2,)),
-            dma((2, 2)),
-            dma((2, 2, 2)),
+            dma((2, CHIPS)),
+            dma((2, 2, CHIPS)),
             pltpu.SemaphoreType.REGULAR,
         ],
         compiler_params=pltpu.CompilerParams(

time: 144 us -> 139 us (0.965)
  Pallas kernels: 142 us -> 137 us
    pallas_call x1, Pallas kernels: 142 us -> 137 us  [shards(): pl.pallas_call(kernel, name='sweep', out_shape=jax.ShapeDtypeStruct((1, S...]
where the time goes in v4:
time: 139 us; the launch traced here: 138 us
  Pallas kernels  137 us (99%)
  local copies, waits for them, and re-layouts  1.47 us (1%)
    pallas_call x1, Pallas kernels, shards(): pl.pallas_call(kernel, name='sweep', out_shape=jax.ShapeDtypeStruct((1, S...  137 us

profile of v4, /device:TPU:1, one launch (start us, length us, event | category | flops | bytes accessed | tf_op | source)
XLA Modules:
  0.0 138.4 jit_solution(11882095949389958259)
XLA Ops:
  0.0 136.9 %sweep.1 = f32[1,16,1024]{2,1,0:T(8,128)} custom-call(f32[1,16,1024]{2,1,0:T(8,128)} %sources.1, f32[1,8,128,128]{3,2,1,0:T(8,128)} %fronts.1, bf16[1,8,128,1024]{3,2,1,0:T(8,128)(2,1)} %down_left.1, bf16[1,8,128,1024]{3,2,1,0:T(8,128)(2,1)} %down_right.1, bf16[1,8,128,1024]{3,2,1,0:T(8,128)(2,1)} %up_left.1, bf16[1,8,128,1024]{3,2,1,0:T(8,128)(2,1)} %up_right.1, ...), custom_call_target="tpu_custom_call" | custom-call | tf_op jit(solution)/shard_map/sweep/pallas_call | solution.py:634
  136.9 1.5 %copy.10 = f32[1,16,1024]{2,1,0:T(8,128)} copy(f32[1,16,1024]{2,1,0:T(8,128)} %sweep.1) | data formatting | bytes 131072

commit v5 on v4

--- a/solution.py
+++ b/solution.py
@@ -515,6 +515,10 @@
         def _():
             make_odd(first)
 
+        @pl.when(early == SLOW + 2)
+        def _():
+            run_odd(first)
+
         make_even(first)
 
         @pl.when(position(first) >= MAKE_EARLY)
@@ -524,7 +528,7 @@
             make_odd(second)
             make_even(second)
 
-        @pl.when(early > SLOW + 1)
+        @pl.when(early > SLOW + 2)
         def _():
             run_odd(first)
 

time: 139 us -> 139 us (level)
  no operation moved by 1% of the time
where the time goes in v5:
time: 139 us; the launch traced here: 138 us
  Pallas kernels  137 us (99%)
  local copies, waits for them, and re-layouts  1.47 us (1%)
    pallas_call x1, Pallas kernels, shards(): pl.pallas_call(kernel, name='sweep', out_shape=jax.ShapeDtypeStruct((1, S...  137 us

profile of v5, /device:TPU:1, one launch (start us, length us, event | category | flops | bytes accessed | tf_op | source)
XLA Modules:
  0.0 138.5 jit_solution(11730792046825279103)
XLA Ops:
  0.0 137.0 %sweep.1 = f32[1,16,1024]{2,1,0:T(8,128)} custom-call(f32[1,16,1024]{2,1,0:T(8,128)} %sources.1, f32[1,8,128,128]{3,2,1,0:T(8,128)} %fronts.1, bf16[1,8,128,1024]{3,2,1,0:T(8,128)(2,1)} %down_left.1, bf16[1,8,128,1024]{3,2,1,0:T(8,128)(2,1)} %down_right.1, bf16[1,8,128,1024]{3,2,1,0:T(8,128)(2,1)} %up_left.1, bf16[1,8,128,1024]{3,2,1,0:T(8,128)(2,1)} %up_right.1, ...), custom_call_target="tpu_custom_call" | custom-call | tf_op jit(solution)/shard_map/sweep/pallas_call | solution.py:638
  137.0 1.5 %copy.10 = f32[1,16,1024]{2,1,0:T(8,128)} copy(f32[1,16,1024]{2,1,0:T(8,128)} %sweep.1) | data formatting | bytes 131072
